TPU v7x, 32 devices: a whole 2x2x4 slice. The times are simulated.
32 devices in a mesh: dp: 16 (over z, y, x), seq: 2 (over core).
Axes of the slice: x: 2, y: 2, z: 4, core: 2. Of those that a mesh axis runs over, the one named last changes fastest.
Arguments:
- hidden_in: float32 [16, 512, 1024], P('dp', 'seq'), may hold values from -6 to 6
- upstream: float32 [16, 512, 1024], P('dp', 'seq'), may hold values from -6 to 6
- in_weight: bfloat16 [1024, 4384], P(('dp', 'seq')), may hold values from -0.1875 to 0.1875
- out_weight: bfloat16 [2048, 1024], P(('dp', 'seq')), may hold values from -0.125 to 0.125
- norm_gain: float32 [1024], replicated, may hold values from 0.5 to 1.5
- conv_weight: float32 [4, 2304], replicated, may hold values from -3 to 3
- conv_bias: float32 [2304], replicated, may hold values from -2 to 2
- step_bias: float32 [32], replicated, may hold values from -9 to -2
- log_rate: float32 [32], replicated, may hold values from 0 to 1.5
- skip_weight: float32 [32], replicated, may hold values from 0.5 to 1.5
- gate_gain: float32 [2048], replicated, may hold values from 0.5 to 1.5
Outputs:
- block_out: float32 [16, 512, 1024], P('dp', 'seq')
- grad_hidden: float32 [16, 512, 1024], P('dp', 'seq')
- grad_in_weight: float32 [1024, 4384], P(('dp', 'seq'))
- grad_out_weight: float32 [2048, 1024], P(('dp', 'seq'))
- grad_norm_gain: float32 [1024], replicated
- grad_conv_weight: float32 [4, 2304], replicated
- grad_conv_bias: float32 [2304], replicated
- grad_step_bias: float32 [32], replicated
- grad_log_rate: float32 [32], replicated
- grad_skip_weight: float32 [32], replicated
- grad_gate_gain: float32 [2048], replicated
All inputs are finite; a program needn't handle non-finite values.
Results may differ from a plain program's by a relative error of at most 0.0077.
Values may be sent and summed in bfloat16 or wider, within the bound.
No kernel may reach another device: no remote copies, remote signals or barrier semaphores. Data moves between devices by JAX's collectives and lax.ppermute only.
A program may use at most 192 MiB of HBM per device.

v0:
```python
import functools

import jax
import jax.numpy as jnp
from jax import lax
from jax.experimental import pallas as pl
from jax.experimental.pallas import tpu as pltpu
from jax.sharding import PartitionSpec as P


D_INNER = 2048
HEADS = 32
HEAD_DIM = 64
STATE = 128
CONVK = 4
GROUP = 256
CONV_CH = 2304
EPS = 1e-05
PRECISE = lax.Precision.HIGHEST
PAD = 8
PLANE = 4
NEVER = -1e30


def pick(x, index, axis):
    return lax.dynamic_index_in_dim(x, index, axis, keepdims=False)


def put(buffer, piece, index, axis):
    return lax.dynamic_update_index_in_dim(buffer, piece, index, axis)


def swapped(x, bit):
    return lax.ppermute(x, "dp", [(i, i ^ bit) for i in range(lax.axis_size("dp"))])


def column_shift(x, steps):
    size = lax.axis_size("dp")
    return lax.ppermute(x, "dp", [(i, (i + PLANE * steps) % size) for i in range(size)])


def seq_shift(x, steps):
    size = lax.axis_size("seq")
    return lax.ppermute(x, "seq", [(i, (i + steps) % size) for i in range(size)])


def seq_sum(x):
    size = lax.axis_size("seq")
    if size == 2:
        return x + seq_shift(x, 1)
    return lax.psum(x, "seq")


def dp_sum(x):
    size = lax.axis_size("dp")
    if size & (size - 1):
        return lax.psum(x, "dp")
    bit = size // 2
    while bit:
        x = x + swapped(x, bit)
        bit //= 2
    return x


def place_kernel(at_ref, *refs, moves, inputs):
    ins, outs, sems = refs[:inputs], refs[inputs:-1], refs[-1]
    copies = []
    for n, (source, columns, target, where) in enumerate(moves):
        src = ins[source] if columns is None else ins[source].at[..., slice(*columns)]
        copies.append(pltpu.make_async_copy(src, outs[target].at[where(at_ref)], sems.at[n]))
    for copy in copies:
        copy.start()
    for copy in copies:
        copy.wait()


def place(at, pieces, shapes, moves):
    return pl.pallas_call(
        functools.partial(place_kernel, moves=moves, inputs=len(pieces)),
        in_specs=[scalar()] + [pl.BlockSpec(memory_space=pl.ANY)] * len(pieces),
        out_specs=[pl.BlockSpec(memory_space=pl.ANY)] * len(shapes),
        out_shape=[jax.ShapeDtypeStruct(shape, pieces[0].dtype) for shape in shapes],
        scratch_shapes=[pltpu.SemaphoreType.DMA((len(moves),))],
    )(at, *pieces)


def gathered(block, cut, gate):
    spot = lax.axis_index("dp")
    at = jnp.stack([spot // PLANE, spot % PLANE // 2, spot % 2])
    height = lax.axis_size("dp") // PLANE
    rows, width = block.shape
    rest = width - cut
    moved = [column_shift(block, steps) for steps in range(1, height)]
    if gate is not None:
        moved, _ = lax.optimization_barrier((moved, gate))
    moves = []
    for k in range(height):
        slot = lambda ref, k=k: (lax.rem(ref[0] + (height - k), height),)
        moves += [(k, (0, cut), 0, slot), (k, (cut, width), 1, slot)]
    left, right = place(at, [block] + moved, [(height, rows, cut), (height, rows, rest)], moves)
    left_near, right_near = swapped(left, 1), swapped(right, 2)
    later = (left_near, right_near)
    every = slice(None)
    left, right = place(
        at,
        [left, left_near, right, right_near],
        [(height, 2, rows, cut), (height, 2, rows, rest)],
        [
            (0, None, 0, lambda ref: (every, ref[2])),
            (1, None, 0, lambda ref: (every, 1 - ref[2])),
            (2, None, 1, lambda ref: (every, ref[1])),
            (3, None, 1, lambda ref: (every, 1 - ref[1])),
        ],
    )
    left_far, right_far = swapped(left, 2), swapped(right, 1)
    left, right = place(
        at,
        [left, left_far, right, right_far],
        [(height, 2, 2, rows, cut), (height, 2, 2, rows, rest)],
        [
            (0, None, 0, lambda ref: (every, ref[1])),
            (1, None, 0, lambda ref: (every, 1 - ref[1])),
            (2, None, 1, lambda ref: (every, every, ref[2])),
            (3, None, 1, lambda ref: (every, every, 1 - ref[2])),
        ],
    )
    return left.reshape(-1, cut), right.reshape(-1, rest), later


def plane_sum(sent, kept, bit):
    at = lax.axis_index("dp")
    height = lax.axis_size("dp") // PLANE
    wide = jnp.float32
    near_bit = 3 - bit
    place = at % PLANE // near_bit % 2
    far = swapped(sent, bit)
    half = (kept.astype(wide) + far.astype(wide)).reshape(height, 2, -1, kept.shape[-1])
    near = swapped(pick(half, 1 - place, 1).astype(sent.dtype), near_bit)
    return pick(half, place, 1) + near.astype(wide), near


def column_sum(column, gate):
    height = lax.axis_size("dp") // PLANE
    tall = lax.axis_index("dp") // PLANE
    sent = column.astype(jnp.bfloat16)
    moved = [column_shift(pick(sent, (tall + k) % height, 0), k) for k in range(1, height)]
    return moved, pick(column, tall, 0), gate


def arrived_sum(parts, gate):
    moved, total, _ = parts
    if gate is not None:
        moved, _ = lax.optimization_barrier((moved, gate))
    for piece in moved:
        total = total + piece.astype(jnp.float32)
    return total


def dot(a, b, over):
    return lax.dot_general(a, b, ((over[0], over[1]), ((), ())), preferred_element_type=jnp.float32)


def spread(columns, width):
    lane = lax.broadcasted_iota(jnp.int32, (1, width), 1)
    out = columns[:, 0:1]
    for head in range(1, width // HEAD_DIM):
        out = jnp.where(lane >= head * HEAD_DIM, columns[:, head : head + 1], out)
    return jnp.broadcast_to(out, (columns.shape[0], width))


def conv_pre(padded_ref, weight, bias, count):
    summed = bias
    for offset in range(CONVK):
        start = PAD - (CONVK - 1) + offset
        summed = summed + weight[offset : offset + 1] * padded_ref[start : start + count, :]
    return summed


def sigmoid(v):
    return 1.0 / (1.0 + jnp.exp(-v))


def causal_mask():
    return lax.broadcasted_iota(jnp.int32, (GROUP, GROUP), 0) >= lax.broadcasted_iota(
        jnp.int32, (GROUP, GROUP), 1
    )


def own_lanes(values, lane):
    return pltpu.roll(values, (values.shape[1] - lane) % values.shape[1], 1)


def folded(values):
    total = values[:, :128]
    for at in range(128, values.shape[1], 128):
        total = total + values[:, at : at + 128]
    return total


def scan_forward(
    normed_ref, wx_ref, wg_ref, pulled_ref, bc_ref, delta_ref, cum_ref, cum_t_ref, par_ref,
    x_ref, gate_ref, mixed_ref, state_ref, sums_ref, pad_ref, *, lead,
):
    count, width = mixed_ref.shape
    bf = jnp.bfloat16
    at = lead + pl.program_id(0) * (width // HEAD_DIM)
    normed = normed_ref[...]
    conv_in = dot(normed, wx_ref[...], ((1,), (0,))).astype(bf)
    gate = dot(normed, wg_ref[...], ((1,), (0,)))
    x_ref[...] = conv_in
    gate_ref[...] = gate
    pad_ref[0:PAD, :] = jnp.zeros((PAD, width), jnp.float32)
    pad_ref[PAD : PAD + count, :] = conv_in.astype(jnp.float32)
    pre = conv_pre(pad_ref, par_ref[0:4, :], par_ref[4:5, :], count)
    acts = pre * sigmoid(pre)
    skip = par_ref[5:6, :]
    causal = causal_mask()
    lane = lax.broadcasted_iota(jnp.int32, (1, 2 * HEAD_DIM), 1)
    state = jnp.zeros((STATE, width), jnp.float32)

    @pl.when(pl.program_id(0) == 0)
    def _():
        sums_ref[...] = jnp.zeros(sums_ref.shape, jnp.float32)

    for group in range(count // GROUP):
        rows = slice(group * GROUP, (group + 1) * GROUP)
        state_ref[group] = state
        b_mat = bc_ref[rows, 0:STATE].astype(bf)
        c_mat = bc_ref[rows, STATE : 2 * STATE].astype(bf)
        inner = dot(c_mat, b_mat, ((1,), (1,)))
        x = acts[rows]
        cum = own_lanes(cum_ref[rows, :], at)
        cum_wide = spread(cum, width)
        last = cum_wide[GROUP - 1 : GROUP, :]
        xd = x * spread(own_lanes(delta_ref[rows, :], at), width)
        xdb = xd.astype(bf)
        y = dot(c_mat, state.astype(bf), ((1,), (0,))) * jnp.exp(cum_wide) + skip * x
        intra = []
        for pair in range(width // (2 * HEAD_DIM)):
            lanes = slice(pair * 2 * HEAD_DIM, (pair + 1) * 2 * HEAD_DIM)
            halves = []
            for head in (2 * pair, 2 * pair + 1):
                gap = jnp.where(causal, cum[:, head : head + 1] - cum_t_ref[pl.ds(at + head, 1), rows], NEVER)
                halves.append(dot((inner * jnp.exp(gap)).astype(bf), xdb[:, lanes], ((1,), (0,))))
            intra.append(jnp.where(lane < HEAD_DIM, halves[0], halves[1]))
        mixed = y + jnp.concatenate(intra, axis=1)
        mixed_ref[rows, :] = mixed
        tail = (xd * jnp.exp(last - cum_wide)).astype(bf)
        state = state * jnp.exp(last) + dot(b_mat, tail, ((0,), (0,)))
        part = gate[rows]
        gated = mixed * part * sigmoid(part)
        sums_ref[rows, 0:128] += folded(gated * gated)
        sums_ref[rows, 128:256] += folded(pulled_ref[rows, :] * par_ref[6:7, :] * gated)


def scan_backward(
    x_ref, gate_ref, mixed_ref, state_ref, pulled_ref, norm_ref, bc_ref, delta_ref, cum_ref, cum_t_ref, par_ref,
    *refs, lead, final,
):
    if final:
        gbc0_ref, gcum0_ref, gdelta0_ref, bcin_ref, step_ref, rate_ref, bcpar_ref = refs[:7]
        refs = refs[7:]
    gx_ref, ggate_ref, gbc_ref, gcum_ref, gdelta_ref, gpar_ref = refs[:6]
    if final:
        gstep_ref, gbcin_ref, gheads_ref, gbcpar_ref = refs[6:10]
    pad_ref, gpad_ref = refs[-2:]
    count, width = x_ref.shape
    bf = jnp.bfloat16
    heads = width // HEAD_DIM
    at = lead + pl.program_id(0) * heads
    pad_ref[0:PAD, :] = jnp.zeros((PAD, width), jnp.float32)
    pad_ref[PAD : PAD + count, :] = x_ref[...].astype(jnp.float32)
    pre = conv_pre(pad_ref, par_ref[0:4, :], par_ref[4:5, :], count)
    sig = sigmoid(pre)
    acts = pre * sig
    slope = sig * (1.0 + pre * (1.0 - sig))
    skip = par_ref[5:6, :]
    gain = par_ref[6:7, :]
    causal = causal_mask()
    lane = lax.broadcasted_iota(jnp.int32, (1, 2 * HEAD_DIM), 1)
    lane_wide = lax.broadcasted_iota(jnp.int32, (1, width), 1) // HEAD_DIM
    lane_all = lax.broadcasted_iota(jnp.int32, (1, 128), 1)
    grad_state = jnp.zeros((STATE, width), jnp.float32)
    gskip = jnp.zeros((1, width), jnp.float32)
    ggain = jnp.zeros((1, width), jnp.float32)

    @pl.when(pl.program_id(0) == 0)
    def _():
        gbc_ref[...] = gbc0_ref[...] if final else jnp.zeros(gbc_ref.shape, jnp.float32)
        gcum_ref[...] = gcum0_ref[...] if final else jnp.zeros(gcum_ref.shape, jnp.float32)
        gdelta_ref[...] = gdelta0_ref[...] if final else jnp.zeros(gdelta_ref.shape, jnp.float32)

    gpad_ref[count : count + PAD, :] = jnp.zeros((PAD, width), jnp.float32)
    for group in reversed(range(count // GROUP)):
        rows = slice(group * GROUP, (group + 1) * GROUP)
        scale, lean = norm_ref[rows, 0:1], norm_ref[rows, 1:2]
        gate, mixed, pulled = gate_ref[rows, :], mixed_ref[rows, :], pulled_ref[rows, :]
        sigma = sigmoid(gate)
        gated = mixed * gate * sigma
        ggain = ggain + jnp.sum(pulled * gated * scale, axis=0, keepdims=True)
        ggated = pulled * gain * scale - gated * lean
        ggate_ref[rows, :] = (ggated * mixed * sigma * (1.0 + gate * (1.0 - sigma))).astype(bf)
        gy = ggated * gate * sigma
        gyb = gy.astype(bf)
        b_mat = bc_ref[rows, 0:STATE].astype(bf)
        c_mat = bc_ref[rows, STATE : 2 * STATE].astype(bf)
        inner = dot(c_mat, b_mat, ((1,), (1,)))
        x = acts[rows]
        cum = own_lanes(cum_ref[rows, :], at)
        cum_wide = spread(cum, width)
        last = cum_wide[GROUP - 1 : GROUP, :]
        decay = jnp.exp(last)
        delta = spread(own_lanes(delta_ref[rows, :], at), width)
        xd = x * delta
        xdb = xd.astype(bf)
        tail = jnp.exp(last - cum_wide)
        state = state_ref[group]
        y = mixed - skip * x
        gye = (gy * jnp.exp(cum_wide)).astype(bf)
        gc = dot(gye, state.astype(bf), ((1,), (1,)))
        gsb = grad_state.astype(bf)
        gxd_tail = dot(b_mat, gsb, ((1,), (0,))) * tail
        gb = dot((xd * tail).astype(bf), gsb, ((1,), (1,)))
        xdf = xdb.astype(jnp.float32)
        glast = jnp.sum(xdf * gxd_tail, axis=0, keepdims=True) + decay * jnp.sum(
            grad_state * state, axis=0, keepdims=True
        )
        grad_state = grad_state * decay + dot(c_mat, gye, ((0,), (0,)))
        ginner = jnp.zeros((GROUP, GROUP), jnp.float32)
        intra = []
        for pair in range(width // (2 * HEAD_DIM)):
            lanes = slice(pair * 2 * HEAD_DIM, (pair + 1) * 2 * HEAD_DIM)
            halves = []
            for side in (0, 1):
                head = 2 * pair + side
                gap = jnp.where(causal, cum[:, head : head + 1] - cum_t_ref[pl.ds(at + head, 1), rows], NEVER)
                fall = jnp.exp(gap)
                weights = (inner * fall).astype(bf)
                own = (lane < HEAD_DIM) if side == 0 else (lane >= HEAD_DIM)
                gyh = jnp.where(own, gy[:, lanes], 0.0).astype(bf)
                ginner = ginner + dot(gyh, xdb[:, lanes], ((1,), (1,))) * fall
                halves.append(dot(weights, gyb[:, lanes], ((0,), (0,))))
            intra.append(jnp.where(lane < HEAD_DIM, halves[0], halves[1]))
        gxd = jnp.concatenate(intra, axis=1) + gxd_tail
        gib = ginner.astype(bf)
        gbc_ref[rows, 0:STATE] += gb + dot(gib, c_mat, ((0,), (0,)))
        gbc_ref[rows, STATE : 2 * STATE] += gc + dot(gib, b_mat, ((1,), (0,)))
        moved = gyb.astype(jnp.float32) * y - xdf * gxd
        drawn = x * gxd
        at_end = lax.broadcasted_iota(jnp.int32, (GROUP, 1), 0) == GROUP - 1
        cums = jnp.zeros((GROUP, 128), jnp.float32)
        draws = jnp.zeros((GROUP, 128), jnp.float32)
        for head in range(heads):
            mine = lane_wide == head
            here = jnp.sum(jnp.where(mine, moved, 0.0), axis=1, keepdims=True)
            end = jnp.sum(jnp.where(mine, glast, 0.0), axis=1, keepdims=True)
            place = lane_all == at + head
            cums = jnp.where(place, here + jnp.where(at_end, end, 0.0), cums)
            draws = jnp.where(place, jnp.sum(jnp.where(mine, drawn, 0.0), axis=1, keepdims=True), draws)
        gcum_ref[rows, :] += cums
        gdelta_ref[rows, :] += draws
        gskip = gskip + jnp.sum(gy * x, axis=0, keepdims=True)
        gpad_ref[rows, :] = (gxd * delta + skip * gy) * slope[rows]
    gpre = gpad_ref[0:count, :]
    total = jnp.zeros((count, width), jnp.float32)
    for offset in range(CONVK):
        ahead = CONVK - 1 - offset
        total = total + par_ref[offset : offset + 1, :] * gpad_ref[ahead : ahead + count, :]
        start = PAD - ahead
        gpar_ref[offset : offset + 1, :] = jnp.sum(
            gpre * pad_ref[start : start + count, :], axis=0, keepdims=True
        )
    gx_ref[...] = total.astype(bf)
    gpar_ref[4:5, :] = jnp.sum(gpre, axis=0, keepdims=True)
    gpar_ref[5:6, :] = gskip
    gpar_ref[6:7, :] = ggain
    gpar_ref[7:8, :] = jnp.zeros((1, width), jnp.float32)
    if not final:
        return

    @pl.when(pl.program_id(0) == pl.num_programs(0) - 1)
    def _():
        below = jnp.where(causal, 1.0, 0.0)
        step_sum = jnp.zeros((1, 128), jnp.float32)
        rate_sum = jnp.zeros((1, 128), jnp.float32)
        for group in range(count // GROUP):
            rows = slice(group * GROUP, (group + 1) * GROUP)
            ga = lax.dot_general(
                below, gcum_ref[rows, :], (((0,), (0,)), ((), ())), precision=PRECISE,
                preferred_element_type=jnp.float32,
            )
            gstep = (ga * rate_ref[0:1, :] + gdelta_ref[rows, :]) * sigmoid(step_ref[rows, :])
            gstep_ref[rows, :] = gstep.astype(bf)
            step_sum = step_sum + jnp.sum(gstep, axis=0, keepdims=True)
            rate_sum = rate_sum + jnp.sum(ga * delta_ref[rows, :], axis=0, keepdims=True)
        gheads_ref[0:1, :] = step_sum
        gheads_ref[1:2, :] = rate_sum * rate_ref[0:1, :]
        gheads_ref[2:8, :] = jnp.zeros((6, 128), jnp.float32)
        for lanes in range(0, 2 * STATE, width):
            cols = slice(lanes, lanes + width)
            pad_ref[PAD : PAD + count, :] = bcin_ref[:, cols].astype(jnp.float32)
            pre = conv_pre(pad_ref, bcpar_ref[0:4, cols], bcpar_ref[4:5, cols], count)
            sig = sigmoid(pre)
            gpre = gbc_ref[:, cols] * sig * (1.0 + pre * (1.0 - sig))
            gpad_ref[0:count, :] = gpre
            total = jnp.zeros((count, width), jnp.float32)
            for offset in range(CONVK):
                ahead = CONVK - 1 - offset
                total = total + bcpar_ref[offset : offset + 1, cols] * gpad_ref[ahead : ahead + count, :]
                start = PAD - ahead
                gbcpar_ref[offset : offset + 1, cols] = jnp.sum(
                    gpre * pad_ref[start : start + count, :], axis=0, keepdims=True
                )
            gbcin_ref[:, cols] = total.astype(bf)
            gbcpar_ref[4:5, cols] = jnp.sum(gpre, axis=0, keepdims=True)
            gbcpar_ref[5:8, cols] = jnp.zeros((3, width), jnp.float32)


def head_block(heads):
    return 4 if heads % 4 == 0 else 2


def fixed(shape):
    return pl.BlockSpec(shape, lambda i: (0,) * len(shape))


def moving(rows, width, at=0):
    return pl.BlockSpec((rows, width), lambda i: (0, i + at))


def mix_forward(part, heads, normed, w_x, w_gate, pulled, bc, delta, cum, cum_t, params):
    count, d_model = normed.shape
    block = head_block(heads)
    width = block * HEAD_DIM
    lead = heads // block * part
    groups = count // GROUP
    whole = heads * HEAD_DIM
    return pl.pallas_call(
        functools.partial(scan_forward, lead=heads * part),
        grid=(heads // block,),
        in_specs=[
            fixed((count, d_model)),
            moving(d_model, width),
            moving(d_model, width),
            moving(count, width, lead),
            fixed((count, 2 * STATE)),
            fixed((count, 128)),
            fixed((count, 128)),
            fixed((128, count)),
            moving(8, width, lead),
        ],
        out_specs=[
            moving(count, width),
            moving(count, width),
            moving(count, width),
            pl.BlockSpec((groups, STATE, width), lambda i: (0, 0, i)),
            fixed((count, 256)),
        ],
        out_shape=[
            jax.ShapeDtypeStruct((count, whole), jnp.bfloat16),
            jax.ShapeDtypeStruct((count, whole), jnp.float32),
            jax.ShapeDtypeStruct((count, whole), jnp.float32),
            jax.ShapeDtypeStruct((groups, STATE, whole), jnp.float32),
            jax.ShapeDtypeStruct((count, 256), jnp.float32),
        ],
        scratch_shapes=[pltpu.VMEM((count + PAD, width), jnp.float32)],
        name="scan",
    )(normed, w_x, w_gate, pulled, bc, delta, cum, cum_t, params)


def mix_backward(part, heads, x, gate, mixed, states, pulled, norms, bc, delta, cum, cum_t, params, *rest):
    count = x.shape[0]
    block = head_block(heads)
    width = block * HEAD_DIM
    lead = heads // block * part
    groups = count // GROUP
    whole = heads * HEAD_DIM
    f32, bf = jnp.float32, jnp.bfloat16
    in_specs = [
        moving(count, width),
        moving(count, width),
        moving(count, width),
        pl.BlockSpec((groups, STATE, width), lambda i: (0, 0, i)),
        moving(count, width, lead),
        fixed((count, 128)),
        fixed((count, 2 * STATE)),
        fixed((count, 128)),
        fixed((count, 128)),
        fixed((128, count)),
        moving(8, width, lead),
    ]
    out_specs = [moving(count, width)] * 2 + [fixed((count, 2 * STATE))] + [fixed((count, 128))] * 2
    out_specs += [moving(8, width)]
    shapes = [((count, whole), bf)] * 2 + [((count, 2 * STATE), f32)] + [((count, 128), f32)] * 2
    shapes += [((8, whole), f32)]
    if rest:
        in_specs += [fixed(v.shape) for v in rest]
        extra = [((count, 128), bf), ((count, 2 * STATE), bf), ((8, 128), f32), ((8, 2 * STATE), f32)]
        out_specs += [fixed(shape) for shape, _ in extra]
        shapes += extra
    return pl.pallas_call(
        functools.partial(scan_backward, lead=heads * part, final=bool(rest)),
        grid=(heads // block,),
        in_specs=in_specs,
        out_specs=out_specs,
        out_shape=[jax.ShapeDtypeStruct(*shape) for shape in shapes],
        scratch_shapes=[pltpu.VMEM((count + PAD, width), f32)] * 2,
        name="unscan",
    )(x, gate, mixed, states, pulled, norms, bc, delta, cum, cum_t, params, *rest)


def halves_kernel(at_ref, *refs, parts, tall):
    left, rights, (sent_ref, kept_ref) = refs[:-parts - 2], refs[-parts - 2 : -2], refs[-2:]
    low = at_ref[0] == 0
    lanes = 0
    for right_ref in rights:
        right = right_ref[...]
        cols = slice(lanes, lanes + right.shape[1])
        lanes += right.shape[1]
        if tall:
            sent_ref[:, cols] = dot(left[0][...], right, ((0,), (0,))).astype(sent_ref.dtype)
            kept_ref[:, cols] = dot(left[1][...], right, ((0,), (0,))).astype(sent_ref.dtype)
        else:
            rows = dot(left[0][...], right, ((0,), (0,)))
            for y in (0, 1):
                first = rows[128 * y : 128 * y + 64]
                second = rows[128 * y + 64 : 128 * y + 128]
                to = slice(64 * y, 64 * y + 64)
                sent_ref[to, cols] = jnp.where(low, second, first).astype(sent_ref.dtype)
                kept_ref[to, cols] = jnp.where(low, first, second).astype(sent_ref.dtype)


def halves(left, rights, bit):
    count, rows = left.shape
    tall = bit == 2
    at = (lax.axis_index("dp") % PLANE // bit % 2).reshape(1)
    if tall:
        lefts = [
            pl.BlockSpec((count, 128), lambda i, at: (0, 2 * i + 1 - at[0])),
            pl.BlockSpec((count, 128), lambda i, at: (0, 2 * i + at[0])),
        ]
    else:
        lefts = [pl.BlockSpec((count, 256), lambda i, at: (0, i))]
    width = sum(v.shape[1] for v in rights)
    shape = jax.ShapeDtypeStruct((rows // 2, width), jnp.bfloat16)
    return pl.pallas_call(
        functools.partial(halves_kernel, parts=len(rights), tall=tall),
        grid_spec=pltpu.PrefetchScalarGridSpec(
            num_scalar_prefetch=1,
            grid=(rows // 256,),
            in_specs=lefts + [pl.BlockSpec(v.shape, lambda i, at: (0, 0)) for v in rights],
            out_specs=[pl.BlockSpec((128, width), lambda i, at: (i, 0))] * 2,
        ),
        out_shape=[shape, shape],
        name="halves",
    )(at, *([left] * len(lefts)), *rights)


def product_kernel(at_ref, *refs, parts):
    lefts, rights, outs = refs[:parts], refs[parts : 2 * parts], refs[2 * parts :]
    rows = outs[0].shape[0]
    for out_ref, place in ((outs[0], at_ref[0]), (outs[1], 1 - at_ref[0])):
        total = 0.0
        for left_ref, right_ref in zip(lefts, rights):
            total = total + dot(left_ref[pl.ds(place * rows, rows), :], right_ref[...], ((1,), (1,)))
        out_ref[...] = total


def product(at, lefts, rights):
    count, width = lefts[0].shape[0], rights[0][0].shape[0]
    block = 256
    shape = jax.ShapeDtypeStruct((count // 2, width), jnp.float32)
    return pl.pallas_call(
        functools.partial(product_kernel, parts=len(lefts)),
        grid_spec=pltpu.PrefetchScalarGridSpec(
            num_scalar_prefetch=1,
            grid=(width // block,),
            in_specs=[pl.BlockSpec(v.shape, lambda i, at: (0, 0)) for v in lefts]
            + [pl.BlockSpec((block, wide), lambda i, at, n=start // wide: (i, n)) for _, wide, start in rights],
            out_specs=[pl.BlockSpec((count // 2, block), lambda i, at: (0, i))] * 2,
        ),
        out_shape=[shape, shape],
        name="product",
    )(at.reshape(1), *lefts, *(v for v, _, _ in rights))


def unzip(at_ref, in_ref, own_ref, other_ref, *, chans, half, heads):
    even = at_ref[0] == 0
    lane = lax.broadcasted_iota(jnp.int32, (1, 128), 1)
    step_at, bc_at = 2 * chans + 2 * STATE, 2 * chans
    kind = own_ref.dtype

    def emit(low, high, to):
        own_ref[:, to : to + 128] = jnp.where(even, low, high).astype(kind)
        other_ref[:, to : to + 128] = jnp.where(even, high, low).astype(kind)

    for source, starts in ((chans, (0, 2 * half + 384)), (0, (half + 128, 3 * half + 384))):
        for at in range(0, chans // 2, 128):
            a = in_ref[:, source + 2 * at : source + 2 * at + 128].astype(jnp.float32)
            b = in_ref[:, source + 2 * at + 128 : source + 2 * at + 256].astype(jnp.float32)
            low = jnp.where(lane < HEAD_DIM, a, pltpu.roll(b, HEAD_DIM, 1))
            high = jnp.where(lane < HEAD_DIM, pltpu.roll(a, HEAD_DIM, 1), b)
            emit(low, high, starts[at // half] + at % half)
    steps = in_ref[:, step_at : step_at + heads]
    row = lax.broadcasted_iota(jnp.int32, (heads, 128), 0)
    col = lax.broadcasted_iota(jnp.int32, (heads, 128), 1)
    sides = [
        dot(steps, jnp.where((row == 2 * col + side) & (col < heads // 2), 1.0, 0.0).astype(kind), ((1,), (0,)))
        for side in (0, 1)
    ]
    emit(sides[0], sides[1], half)
    bc = in_ref[:, bc_at:step_at]
    own_ref[:, 2 * half + 128 : 2 * half + 384] = bc
    other_ref[:, 2 * half + 128 : 2 * half + 384] = bc


def zipped(at_ref, own1_ref, other1_ref, own2_ref, other2_ref, out_ref, *, chans, half, heads):
    even = at_ref[0] == 0
    lane = lax.broadcasted_iota(jnp.int32, (1, 128), 1)
    bc_at, step_at = 2 * chans, 2 * chans + 2 * STATE
    for target, lead in ((chans, 0), (0, 1)):
        for at in range(0, chans // 2, 128):
            second = at >= half
            to = at % half + lead * (half if second else half + 128)
            own_ref, other_ref = (own2_ref, other2_ref) if second else (own1_ref, other1_ref)
            own, other = own_ref[:, to : to + 128], other_ref[:, to : to + 128]
            low, high = jnp.where(even, own, other), jnp.where(even, other, own)
            out_ref[:, target + 2 * at : target + 2 * at + 128] = jnp.where(
                lane < HEAD_DIM, low, pltpu.roll(high, HEAD_DIM, 1)
            )
            out_ref[:, target + 2 * at + 128 : target + 2 * at + 256] = jnp.where(
                lane < HEAD_DIM, pltpu.roll(low, HEAD_DIM, 1), high
            )
    cols = slice(2 * half + 128, 2 * half + 384)
    out_ref[:, bc_at:step_at] = own1_ref[:, cols] + other1_ref[:, cols]
    row = lax.broadcasted_iota(jnp.int32, (128, heads), 0)
    col = lax.broadcasted_iota(jnp.int32, (128, heads), 1)
    own, other = own1_ref[:, half : half + 128], other1_ref[:, half : half + 128]
    total = 0.0
    for side, values in ((0, jnp.where(even, own, other)), (1, jnp.where(even, other, own))):
        choice = jnp.where((col == 2 * row + side) & (row < heads // 2), 1.0, 0.0)
        total = total + lax.dot_general(
            values, choice, (((1,), (0,)), ((), ())), precision=PRECISE, preferred_element_type=jnp.float32
        )
    out_ref[:, step_at : step_at + heads] = total


def scalar():
    return pl.BlockSpec(memory_space=pltpu.SMEM)


def full():
    return pl.BlockSpec(memory_space=pltpu.VMEM)


def unzip_columns(at, rows, half):
    shape = jax.ShapeDtypeStruct((rows.shape[0], 4 * half + 384), rows.dtype)
    return pl.pallas_call(
        functools.partial(unzip, chans=D_INNER, half=half, heads=HEADS),
        in_specs=[scalar(), full()],
        out_specs=[full(), full()],
        out_shape=[shape, shape],
        name="unzip",
    )(at.reshape(1), rows)


def zip_columns(at, own1, other1, own2, other2, half):
    return pl.pallas_call(
        functools.partial(zipped, chans=D_INNER, half=half, heads=HEADS),
        in_specs=[scalar()] + [full()] * 4,
        out_specs=full(),
        out_shape=jax.ShapeDtypeStruct((own1.shape[0], D_INNER + CONV_CH + HEADS), jnp.float32),
        name="zip",
    )(at.reshape(1), own1, other1, own2, other2)


def rms_scale(values, gain):
    return values * lax.rsqrt(jnp.mean(values * values, axis=-1, keepdims=True) + EPS) * gain


def conv_act(values, conv_weight, conv_bias):
    count = values.shape[0]
    extended = jnp.concatenate([jnp.zeros((CONVK - 1, values.shape[1]), jnp.float32), values], axis=0)
    summed = conv_bias[None, :] + conv_weight[0][None, :] * extended[0:count]
    for offset in range(1, CONVK):
        summed = summed + conv_weight[offset][None, :] * extended[offset : offset + count]
    return jax.nn.silu(summed)


class Split:
    def __init__(self, out_rows, d_model):
        self.peers = lax.axis_size("seq")
        self.at = lax.axis_index("seq")
        blocks = lax.axis_size("dp")
        self.staged = out_rows == HEAD_DIM and blocks * HEAD_DIM == d_model and blocks % PLANE == 0 and self.peers == 2
        self.outer = blocks if self.staged else 1

    def view(self, v):
        return v.reshape(v.shape[:-1] + (self.outer, self.peers, v.shape[-1] // (self.outer * self.peers)))

    def own(self, v, at=None):
        part = pick(self.view(v), self.at if at is None else at, v.ndim)
        return part.reshape(v.shape[:-1] + (-1,))

    def place(self, whole, part, at=None):
        view = self.view(whole)
        piece = part.reshape(view.shape[:-2] + view.shape[-1:])
        return put(view, piece, self.at if at is None else at, whole.ndim).reshape(whole.shape)

    def placed(self, part):
        return self.place(jnp.zeros(part.shape[:-1] + (part.shape[-1] * self.peers,), part.dtype), part)

    def exchange(self, piece_for):
        pieces = [(self.at, piece_for(self.at))]
        for steps in range(1, self.peers):
            sent = piece_for((self.at + steps) % self.peers)
            pieces.append(((self.at - steps) % self.peers, seq_shift(sent, steps)))
        return pieces

    def scatter_rows(self, x):
        rows = x.reshape((self.peers, x.shape[0] // self.peers) + x.shape[1:])
        total = 0.0
        for _, piece in self.exchange(lambda to: pick(rows, to, 0)):
            total = total + piece
        return total


def per_device(
    hidden_in, upstream, in_weight, out_weight, norm_gain, conv_weight, conv_bias,
    step_bias, log_rate, skip_weight, gate_gain,
):
    bf = jnp.bfloat16
    split = Split(*out_weight.shape)
    peers, at = split.peers, split.at
    stream, grad_top = hidden_in[0], upstream[0]
    own_rows, d_model = stream.shape
    count = own_rows * peers
    groups = count // GROUP
    heads = HEADS // peers
    inner = D_INNER // peers
    half_heads = heads // 2
    half = inner // 2
    lanes = -(-heads // 128) * 128

    def in_columns(rows):
        x = split.own(rows[:, D_INNER : 2 * D_INNER])
        gate = split.own(rows[:, :D_INNER])
        bc = rows[:, 2 * D_INNER : D_INNER + CONV_CH]
        steps = split.own(rows[:, D_INNER + CONV_CH :])
        blank = jnp.zeros((rows.shape[0], lanes - heads), rows.dtype)
        return (
            jnp.concatenate([x[:, :half], steps, blank], axis=1),
            jnp.concatenate([gate[:, :half], bc], axis=1),
            x[:, half:],
            gate[:, half:],
        )

    first_cut = half + lanes
    first_width = first_cut + half + 2 * STATE
    if split.staged:
        own, other = unzip_columns(at, in_weight, half)
        arrived = seq_shift(other, 1)
        here = lambda ref: (ref[0],)
        there = lambda ref: (1 - ref[0],)
        total = own.shape[1]
        block_first, block_second = place(
            at.reshape(1),
            [own, arrived],
            [(peers, own.shape[0], first_width), (peers, own.shape[0], total - first_width)],
            [
                (source, columns, target, where)
                for source, where in ((0, here), (1, there))
                for target, columns in ((0, (0, first_width)), (1, (first_width, total)))
            ],
        )
        block_first = block_first.reshape(-1, first_width)
        block_second = block_second.reshape(-1, total - first_width)

    normed_own = rms_scale(stream, norm_gain).astype(bf)
    both = jnp.concatenate([normed_own, grad_top.astype(bf)], axis=1)
    half_model = d_model // 2
    if split.staged:
        arrived = seq_shift(both, 1)
        spans = ((0, d_model), (d_model, d_model + half_model), (d_model + half_model, 2 * d_model))
        normed, top_left, top_right = place(
            at.reshape(1),
            [both, arrived],
            [(peers, own_rows, stop - start) for start, stop in spans],
            [
                (source, span, target, where)
                for source, where in ((0, here), (1, there))
                for target, span in enumerate(spans)
            ],
        )
        normed, top_left, top_right = (v.reshape(count, -1) for v in (normed, top_left, top_right))
    else:
        tokens = jnp.zeros((peers,) + both.shape, bf)
        for origin, part in split.exchange(lambda to: both):
            tokens = put(tokens, part, origin, 0)
        tokens = tokens.reshape(count, -1)
        normed, top = tokens[:, :d_model], tokens[:, d_model:]
        top_left, top_right = top[:, :half_model], top[:, half_model:]

    if split.staged:
        out_left, out_right, gate = gathered(out_weight, d_model // 2, None)
        x_first, gate_first, gate = gathered(block_first, first_cut, gate)
        x_second, gate_second, _ = gathered(block_second, half, gate)
    else:
        in_all = lax.all_gather(in_weight, ("dp", "seq"), axis=0, tiled=True)
        x_first, gate_first, x_second, gate_second = in_columns(in_all)
        out_all = split.own(lax.all_gather(out_weight, ("dp", "seq"), axis=0, tiled=True).T).T
        out_left, out_right = out_all[:, : d_model // 2], out_all[:, d_model // 2 :]

    own_bias = split.own(step_bias)
    rates = -jnp.exp(split.own(log_rate))
    own_gain = split.own(gate_gain)
    conv_x = split.own(conv_weight[:, :D_INNER])
    params = jnp.concatenate(
        [
            conv_x,
            split.own(conv_bias[:D_INNER])[None],
            jnp.repeat(split.own(skip_weight), HEAD_DIM)[None],
            own_gain[None],
            jnp.zeros((1, inner), jnp.float32),
        ],
        axis=0,
    )
    tri = (jnp.arange(GROUP)[:, None] >= jnp.arange(GROUP)[None, :]).astype(jnp.float32)

    step_raw = dot(normed, x_first[:, half:], ((1,), (0,)))
    step_in = step_raw + jnp.pad(own_bias, (0, lanes - heads))[None, :]
    all_rates = jnp.pad(rates, (0, lanes - heads))[None, :]
    deltas = jax.nn.softplus(step_in)
    cum = jnp.einsum(
        "ts,gsh->gth", tri, (deltas * all_rates).reshape(groups, GROUP, lanes), precision=PRECISE
    ).reshape(count, lanes)
    cum_t = cum.T
    bc_in = dot(normed, gate_first[:, half:], ((1,), (0,))).astype(bf)
    bc_params = jnp.concatenate(
        [conv_weight[:, D_INNER:], conv_bias[None, D_INNER:], jnp.zeros((3, 2 * STATE), jnp.float32)], axis=0
    )
    bc = conv_act(bc_in.astype(jnp.float32), conv_weight[:, D_INNER:], conv_bias[D_INNER:])

    pulled = dot(top_left, out_left, ((1,), (1,))) + dot(top_right, out_right, ((1,), (1,)))
    saved = []
    for part, (w_x, w_gate) in enumerate(((x_first, gate_first), (x_second, gate_second))):
        saved.append(mix_forward(part, half_heads, normed, w_x, w_gate, pulled, bc, deltas, cum, cum_t, params))
    sums = saved[0][4] + saved[1][4]
    sums = jnp.stack([jnp.sum(sums[:, :128], axis=1), jnp.sum(sums[:, 128:], axis=1)])
    sums = seq_sum(sums)
    scale = lax.rsqrt(sums[0] / D_INNER + EPS)
    lean = sums[1] * scale * scale * scale / D_INNER
    norms = jnp.pad(jnp.stack([scale, lean], axis=1), ((0, 0), (0, 126)))

    normed_out = jnp.concatenate(
        [
            (mixed * jax.nn.silu(gate) * scale[:, None] * own_gain[None, part * half : (part + 1) * half]).astype(bf)
            for part, (_, gate, mixed, _, _) in enumerate(saved)
        ],
        axis=1,
    )
    if split.staged:
        out_halves = halves(normed_out, (top_left, top_right), 2)
        out_parts = column_sum(*plane_sum(*out_halves, 2))

    gx1, ggate1, *carried, gpar1 = mix_backward(
        1, half_heads, *saved[1][:4], pulled, norms, bc, deltas, cum, cum_t, params
    )
    if split.staged:
        second_halves = halves(normed, (gx1, ggate1), 1)
        second_parts = column_sum(*plane_sum(*second_halves, 1))
    gx0, ggate0, _, _, _, gpar0, gstep, gbc, gheads, gbc_par = mix_backward(
        0, half_heads, *saved[0][:4], pulled, norms, bc, deltas, cum, cum_t, params,
        *carried, bc_in, step_in, jnp.broadcast_to(all_rates, (8, lanes)), bc_params,
    )
    grads = (gx0, gstep, ggate0, gbc, gx1, ggate1)
    columns = (
        (x_first, half, 0), (x_first, lanes, half), (gate_first, half, 0), (gate_first, 2 * STATE, half),
        (x_second, half, 0), (gate_second, half, 0),
    )
    if split.staged:
        left_halves = halves(normed, (gx0, gstep), 2)
        right_halves = halves(normed, (ggate0, gbc), 1)
        left, near_left = plane_sum(*left_halves, 2)
        right, near_right = plane_sum(*right_halves, 1)
        gate = (near_left, near_right)
        first_parts = column_sum(jnp.concatenate([left, right], axis=-1), gate)
        kept, sent = product(at, grads, columns)
        grad_normed = kept + seq_shift(sent, 1)
    else:
        grad_normed = 0.0
        for side, (weight, width, start) in zip(grads, columns):
            grad_normed = grad_normed + dot(side, weight[:, start : start + width], ((1,), (1,)))
        grad_normed = split.scatter_rows(grad_normed)

    def block_rows(to):
        rows = lax.dynamic_slice_in_dim(normed_out, to * own_rows, own_rows, 0)
        return jnp.concatenate([dot(rows, side, ((1,), (0,))) for side in (out_left, out_right)], axis=1)

    block_out = stream
    for _, piece in split.exchange(block_rows):
        block_out = block_out + piece
    _, norm_back = jax.vjp(rms_scale, stream, norm_gain)
    grad_stream, grad_norm_gain = norm_back(grad_normed)

    small = (gpar0, gpar1, gbc_par, gheads, grad_norm_gain)
    packed = dp_sum(jnp.concatenate([v.reshape(-1, 128) for v in small]))
    other_packed = None
    if split.staged:
        other_packed = seq_shift(packed, 1)
    summed = []
    for source in (packed, other_packed):
        offset, parts = 0, []
        for v in small:
            parts.append(None if source is None else source[offset : offset + v.size // 128].reshape(v.shape))
            offset += v.size // 128
        summed.append(parts)
    mine, theirs = summed
    shared = [None, None]
    for n, k in ((0, 2), (1, 4)):
        shared[n] = mine[k] + theirs[k] if split.staged else lax.psum(mine[k], "seq")

    def spread_rows(pick_row):
        own_row = pick_row(mine)
        if split.staged:
            other_row = pick_row(theirs)
            view = own_row.shape[:-1] + (split.outer, own_row.shape[-1] // split.outer)
            own_row, other_row = own_row.reshape(view), other_row.reshape(view)
            low = jnp.where(at == 0, own_row, other_row)
            high = jnp.where(at == 0, other_row, own_row)
            return jnp.stack([low, high], axis=-2).reshape(view[:-2] + (-1,))
        return lax.psum(split.placed(own_row), "seq")

    rows = spread_rows(lambda v: jnp.concatenate([v[0], v[1]], axis=1))
    head_rows = spread_rows(lambda v: v[3][:, :heads])
    grad_bc_par = shared[0]
    small_out = (
        jnp.concatenate([rows[:CONVK], grad_bc_par[:CONVK]], axis=1),
        jnp.concatenate([rows[CONVK], grad_bc_par[CONVK]]),
        head_rows[0],
        head_rows[1],
        jnp.sum(rows[CONVK + 1].reshape(HEADS, HEAD_DIM), axis=1),
        rows[CONVK + 2],
    )

    if split.staged:
        out_share = arrived_sum(out_parts, gate)
        pairs = []
        for parts, after in ((first_parts, None), (second_parts, gate)):
            share = arrived_sum(parts, after)
            pair = share.reshape(peers, -1, share.shape[-1])
            pairs += [pick(pair, at, 0), seq_shift(pick(pair, 1 - at, 0), 1)]
        in_share = zip_columns(at, *pairs, half)
    else:
        empty = jnp.zeros((d_model, D_INNER), jnp.float32)
        x_low, step_low, gate_low, bc_low, x_high, gate_high = (dot(normed, side, ((0,), (0,))) for side in grads)
        in_share = jnp.concatenate(
            [
                split.place(empty, jnp.concatenate([gate_low, gate_high], axis=1)),
                split.place(empty, jnp.concatenate([x_low, x_high], axis=1)),
                bc_low,
                split.placed(step_low[:, :heads]),
            ],
            axis=1,
        )
        in_share = lax.psum_scatter(in_share, ("dp", "seq"), scatter_dimension=0, tiled=True)
        grad_out = dot(normed_out, jnp.concatenate([top_left, top_right], axis=1), ((0,), (0,)))
        out_share = lax.psum_scatter(
            split.placed(grad_out.T).T, ("dp", "seq"), scatter_dimension=0, tiled=True
        )

    return (
        block_out[None], (grad_top + grad_stream)[None], in_share, out_share, shared[1], *small_out,
    )


def solution(mesh):
    tokens, rows, whole = P("dp", "seq", None), P(("dp", "seq"), None), P()
    return jax.shard_map(
        per_device,
        mesh=mesh,
        in_specs=(tokens, tokens, rows, rows) + (whole,) * 7,
        out_specs=(tokens, tokens, rows, rows) + (whole,) * 7,
        check_vma=False,
    )
```

profile of v0, /device:TPU:14, one launch (start us, length us, event | category | flops | bytes accessed | tf_op | source)
XLA Modules:
  0.0 761.9 jit_solution(15873214176576491697)
XLA Ops:
  0.7 2.7 collective-permute-start.6
  11.9 10.6 %shard_map.195 = (bf16[2,32,1408]{2,1,0:T(8,128)(2,1)}, bf16[2,32,1024]{2,1,0:T(8,128)(2,1)}) custom-call(s32[1]{0:T(128)} %bitcast.1.at_ref, bf16[32,2432]{1,0:T(8,128)(2,1)} %get-tuple-element.82.refs_0_, bf16[32,2432]{1,0:T(8,128)(2,1)} %copy-done.33), custom_call_target="tpu_custom_call" | custom-call | tf_op jit(solution)/shard_map/pallas_call | solution.py:78
  25.8 17.7 %shard_map.196 = (bf16[4,64,512]{2,1,0:T(8,128)(2,1)}, bf16[4,64,512]{2,1,0:T(8,128)(2,1)}) custom-call(s32[3]{0:T(128)} %pad_add_fusion.at_ref, bf16[64,1024]{1,0:T(8,128)(2,1)} %refs_0_.1, bf16[64,1024]{1,0:T(8,128)(2,1)} %collective-permute-done.5.refs_1_, bf16[64,1024]{1,0:T(8,128)(2,1)} %collective-permute-done.6.refs_2_, ...), custom_call_target="tpu_custom_call" | custom-call | tf_op jit(solution)/shard_map/pallas_call | solution.py:78
  46.4 6.6 collective-permute-done.3.refs_2_
  53.0 7.2 collective-permute-start.18
  60.9 23.7 %shard_map.197 = (bf16[4,64,640]{2,1,0:T(8,128)(2,1)}, bf16[4,64,768]{2,1,0:T(8,128)(2,1)}) custom-call(s32[3]{0:T(128)} %pad_add_fusion.at_ref, bf16[64,1408]{1,0:T(8,128)(2,1)} %bitcast.225, bf16[64,1408]{1,0:T(8,128)(2,1)} %copy-done.32, bf16[64,1408]{1,0:T(8,128)(2,1)} %copy-done.31, bf16[64,1408]{1,0:T(8,128)(2,1)} %copy-done.29), custom_call_target="tpu_custom_call" | custom-call | tf_op jit(solution)/shard_map/pallas_call | solution.py:78
  88.6 33.6 %shard_map.200 = (bf16[4,2,64,512]{3,2,1,0:T(8,128)(2,1)}, bf16[4,2,64,512]{3,2,1,0:T(8,128)(2,1)}) custom-call(s32[3]{0:T(128)} %pad_add_fusion.at_ref, bf16[4,64,512]{2,1,0:T(8,128)(2,1)} %get-tuple-element.85.refs_0_, bf16[4,64,512]{2,1,0:T(8,128)(2,1)} %copy-done.26, bf16[4,64,512]{2,1,0:T(8,128)(2,1)} %get-tuple-element.86.refs_2_, ...), custom_call_target="tpu_custom_call" | custom-call | tf_op jit(solution)/shard_map/pallas_call | solution.py:78
  134.7 17.7 %shard_map.202 = (bf16[4,64,512]{2,1,0:T(8,128)(2,1)}, bf16[4,64,512]{2,1,0:T(8,128)(2,1)}) custom-call(s32[3]{0:T(128)} %pad_add_fusion.at_ref, bf16[64,1024]{1,0:T(8,128)(2,1)} %bitcast.231, bf16[64,1024]{1,0:T(8,128)(2,1)} %copy-done.35, bf16[64,1024]{1,0:T(8,128)(2,1)} %collective-permute-done.17.refs_2_, bf16[64,1024]{1,0:T(8,128)(2,1)} %copy-done.34), custom_call_target="tpu_custom_call" | custom-call | tf_op jit(solution)/shard_map/pallas_call | solution.py:78
  157.0 45.5 %shard_map.198 = (bf16[4,2,64,640]{3,2,1,0:T(8,128)(2,1)}, bf16[4,2,64,768]{3,2,1,0:T(8,128)(2,1)}) custom-call(s32[3]{0:T(128)} %pad_add_fusion.at_ref, bf16[4,64,640]{2,1,0:T(8,128)(2,1)} %get-tuple-element.90.refs_0_, bf16[4,64,640]{2,1,0:T(8,128)(2,1)} %collective-permute-done.10.refs_1_, bf16[4,64,768]{2,1,0:T(8,128)(2,1)} %get-tuple-element.91.refs_2_, ...), custom_call_target="tpu_custom_call" | custom-call | tf_op jit(solution)/shard_map/pallas_call | solution.py:78
  206.2 65.3 %shard_map.201 = (bf16[4,2,2,64,512]{4,3,2,1,0:T(8,128)(2,1)}, bf16[4,2,2,64,512]{4,3,2,1,0:T(8,128)(2,1)}) custom-call(s32[3]{0:T(128)} %pad_add_fusion.at_ref, bf16[4,2,64,512]{3,2,1,0:T(8,128)(2,1)} %get-tuple-element.97.refs_0_, bf16[4,2,64,512]{3,2,1,0:T(8,128)(2,1)} %copy-done.22, bf16[4,2,64,512]{3,2,1,0:T(8,128)(2,1)} %get-tuple-element.98.refs_2_, ...), custom_call_target="tpu_custom_call" | custom-call | tf_op jit(solution)/shard_map/pallas_call | solution.py:78
  271.6 33.7 %shard_map.203 = (bf16[4,2,64,512]{3,2,1,0:T(8,128)(2,1)}, bf16[4,2,64,512]{3,2,1,0:T(8,128)(2,1)}) custom-call(s32[3]{0:T(128)} %pad_add_fusion.at_ref, bf16[4,64,512]{2,1,0:T(8,128)(2,1)} %get-tuple-element.109.refs_0_, bf16[4,64,512]{2,1,0:T(8,128)(2,1)} %collective-permute-done.19.refs_1_, bf16[4,64,512]{2,1,0:T(8,128)(2,1)} %get-tuple-element.110.refs_2_, ...), custom_call_target="tpu_custom_call" | custom-call | tf_op jit(solution)/shard_map/pallas_call | solution.py:78
  309.0 64.7 %shard_map.194 = (bf16[2,256,1024]{2,1,0:T(8,128)(2,1)}, bf16[2,256,512]{2,1,0:T(8,128)(2,1)}, bf16[2,256,512]{2,1,0:T(8,128)(2,1)}) custom-call(s32[1]{0:T(128)} %bitcast.1.at_ref, bf16[256,2048]{1,0:T(8,128)(2,1)} %copy-done.7, bf16[256,2048]{1,0:T(8,128)(2,1)} %copy-done.15), custom_call_target="tpu_custom_call" | custom-call | tf_op jit(solution)/shard_map/pallas_call | solution.py:78
  377.8 89.3 %shard_map.199 = (bf16[4,2,2,64,640]{4,3,2,1,0:T(8,128)(2,1)}, bf16[4,2,2,64,768]{4,3,2,1,0:T(8,128)(2,1)}) custom-call(s32[3]{0:T(128)} %pad_add_fusion.at_ref, bf16[4,2,64,640]{3,2,1,0:T(8,128)(2,1)} %get-tuple-element.92.refs_0_, bf16[4,2,64,640]{3,2,1,0:T(8,128)(2,1)} %collective-permute-done.12.refs_1_, ...), custom_call_target="tpu_custom_call" | custom-call | tf_op jit(solution)/shard_map/pallas_call | solution.py:78
  474.0 8.4 %scan.2 = (bf16[512,512]{1,0:T(8,128)(2,1)}, f32[512,512]{1,0:T(8,128)}, f32[512,512]{1,0:T(8,128)}, f32[2,128,512]{2,1,0:T(8,128)}, f32[512,256]{1,0:T(8,128)}) custom-call(bf16[512,1024]{1,0:T(8,128)(2,1)} %bitcast.178, bf16[1024,640]{1,0:T(8,128)(2,1)} %bitcast.191, bf16[1024,768]{1,0:T(8,128)(2,1)} %bitcast.187, ...), custom_call_target="tpu_custom_call" | custom-call | tf_op jit(solution)/shard_map/scan/pallas_call | solution.py:438
  482.4 65.3 %shard_map.204 = (bf16[4,2,2,64,512]{4,3,2,1,0:T(8,128)(2,1)}, bf16[4,2,2,64,512]{4,3,2,1,0:T(8,128)(2,1)}) custom-call(s32[3]{0:T(128)} %pad_add_fusion.at_ref, bf16[4,2,64,512]{3,2,1,0:T(8,128)(2,1)} %get-tuple-element.111.refs_0_, bf16[4,2,64,512]{3,2,1,0:T(8,128)(2,1)} %collective-permute-done.21.refs_1_, ...), custom_call_target="tpu_custom_call" | custom-call | tf_op jit(solution)/shard_map/pallas_call | solution.py:78
  547.8 8.5 %scan.3 = (bf16[512,512]{1,0:T(8,128)(2,1)}, f32[512,512]{1,0:T(8,128)}, f32[512,512]{1,0:T(8,128)}, f32[2,128,512]{2,1,0:T(8,128)}, f32[512,256]{1,0:T(8,128)}) custom-call(bf16[512,1024]{1,0:T(8,128)(2,1)} %bitcast.179, bf16[1024,512]{1,0:T(8,128)(2,1)} %bitcast.205, bf16[1024,512]{1,0:T(8,128)(2,1)} %bitcast.207, ...), custom_call_target="tpu_custom_call" | custom-call | tf_op jit(solution)/shard_map/scan/pallas_call | solution.py:438
  566.0 12.6 %unscan.2 = (bf16[512,512]{1,0:T(8,128)(2,1)}, bf16[512,512]{1,0:T(8,128)(2,1)}, f32[512,256]{1,0:T(8,128)}, f32[512,128]{1,0:T(8,128)}, f32[512,128]{1,0:T(8,128)}, /*index=5*/f32[8,512]{1,0:T(8,128)}) custom-call(bf16[512,512]{1,0:T(8,128)(2,1)} %get-tuple-element.120.x_ref, f32[512,512]{1,0:T(8,128)} %get-tuple-element.117.gate_ref, ...), custom_call_target="tpu_custom_call" | custom-call | tf_op jit(solution)/shard_map/unscan/pallas_call | solution.py:501
  579.2 16.1 %unscan.3 = (bf16[512,512]{1,0:T(8,128)(2,1)}, bf16[512,512]{1,0:T(8,128)(2,1)}, f32[512,256]{1,0:T(8,128)}, f32[512,128]{1,0:T(8,128)}, f32[512,128]{1,0:T(8,12...) custom-call(bf16[512,512]{1,0:T(8,128)(2,1)} %get-tuple-element.118., ...), custom_call_target="tpu_custom_call" | custom-call | tf_op jit(solution)/shard_map/unscan/pallas_call | solution.py:501
  596.8 4.8 halves.6
  601.6 4.5 halves.5
  606.1 7.1 product.1
  613.2 4.4 halves.4
  617.7 4.9 halves.7
  628.9 11.4 %collective-permute-done.26 = bf16[512,640]{1,0:T(8,128)(2,1)S(1)} collective-permute-done((bf16[512,640]{1,0:T(8,128)(2,1)}, bf16[512,640]{1,0:T(8,128)(2,1)S(1)}, u32[]{:S(2)}, u32[]{:S(2)}) %collective-permute-start.26) | collective-permute-done | bytes 655392 | tf_op jit(solution)/shard_map/ppermute | solution.py:34
  640.6 3.4 collective-permute-done.28
  644.8 27.6 %collective-permute-done.27 = bf16[4,64,640]{2,1,0:T(8,128)(2,1)S(1)} collective-permute-done((bf16[4,64,640]{2,1,0:T(8,128)(2,1)S(1)}, bf16[4,64,640]{2,1,0:T(8,128)(2,1)S(1)}, u32[]{:S(2)}, u32[]{:S(2)}) %collective-permute-start.27) | collective-permute-done | bytes 327712 | tf_op jit(solution)/shard_map/ppermute | solution.py:34
  679.7 3.6 collective-permute-done.45
  688.9 5.8 collective-permute-done.47
  740.1 2.7 collective-permute-start.43
  744.7 2.9 collective-permute-start.42
  747.6 5.1 collective-permute-done.36
  753.5 3.0 collective-permute-done.44
  (324 shorter events, 139.6 us)
Async XLA Ops:
  0.7 25.1 %collective-permute-start.6 = (bf16[64,1024]{1,0:T(8,128)(2,1)}, bf16[64,1024]{1,0:T(8,128)(2,1)}, u32[]{:S(2)}, u32[]{:S(2)}) collective-permute-start(bf16[64,1024]{1,0:T(8,128)(2,1)} %refs_0_.1), channel_id=1, source_target_pairs={{0,16},{2,18},{4,20},{6,22},{8,24},{10,26},{12,28},{14,30},{16,0},... | collective-permute-start | bytes 393224 | tf_op jit(solution)/shard_map/ppermute | solution.py:39
  3.3 22.5 %collective-permute-start.5 = (bf16[64,1024]{1,0:T(8,128)(2,1)}, bf16[64,1024]{1,0:T(8,128)(2,1)}, u32[]{:S(2)}, u32[]{:S(2)}) collective-permute-start(bf16[64,1024]{1,0:T(8,128)(2,1)} %refs_0_.1), channel_id=1, source_target_pairs={{0,8},{2,10},{4,12},{6,14},{8,16},{10,18},{12,20},{14,22},{16,24},... | collective-permute-start | bytes 393224 | tf_op jit(solution)/shard_map/ppermute | solution.py:39
  3.3 22.5 %collective-permute-start.7 = (bf16[64,1024]{1,0:T(8,128)(2,1)}, bf16[64,1024]{1,0:T(8,128)(2,1)}, u32[]{:S(2)}, u32[]{:S(2)}) collective-permute-start(bf16[64,1024]{1,0:T(8,128)(2,1)} %refs_0_.1), channel_id=1, source_target_pairs={{0,24},{2,26},{4,28},{6,30},{8,0},{10,2},{12,4},{14,6},{16,8},{18,... | collective-permute-start | bytes 393224 | tf_op jit(solution)/shard_map/ppermute | solution.py:39
  22.5 22.2 %collective-permute-start.4 = (bf16[64,1408]{1,0:T(8,128)(2,1)}, bf16[64,1408]{1,0:T(8,128)(2,1)S(1)}, u32[]{:S(2)}, u32[]{:S(2)}) collective-permute-start(bf16[64,1408]{1,0:T(8,128)(2,1)} %bitcast.224), channel_id=1, source_target_pairs={{0,24},{2,26},{4,28},{6,30},{8,0},{10,2},{12,4},{14,6},{16,8},{18,... | collective-permute-start | bytes 540680 | tf_op jit(solution)/shard_map/ppermute | solution.py:39
  24.9 283.2 %collective-permute-start = (bf16[256,2048]{1,0:T(8,128)(2,1)S(1)}, bf16[256,2048]{1,0:T(8,128)(2,1)S(1)}, u32[]{:S(2)}, u32[]{:S(2)}) collective-permute-start(bf16[256,2048]{1,0:T(8,128)(2,1)S(1)} %pad_maximum_fusion.2.refs_0_), channel_id=1, source_target_pairs={{0,1},{1,0},{2,3},{3,2},{4,5},{5,4},{6,7},{7,6},{8,9},{9,8},{10,11... | collective-permute-start | bytes 3145736 | tf_op jit(solution)/shard_map/ppermute | solution.py:44
  53.0 34.1 %collective-permute-start.18 = (bf16[64,1024]{1,0:T(8,128)(2,1)}, bf16[64,1024]{1,0:T(8,128)(2,1)S(1)}, u32[]{:S(2)}, u32[]{:S(2)}) collective-permute-start(bf16[64,1024]{1,0:T(8,128)(2,1)} %bitcast.228), channel_id=1, source_target_pairs={{0,24},{2,26},{4,28},{6,30},{8,0},{10,2},{12,4},{14,6},{16,8},{18,... | collective-permute-start | bytes 393224 | tf_op jit(solution)/shard_map/ppermute | solution.py:39
  60.2 61.9 %collective-permute-start.17 = (bf16[64,1024]{1,0:T(8,128)(2,1)}, bf16[64,1024]{1,0:T(8,128)(2,1)}, u32[]{:S(2)}, u32[]{:S(2)}) collective-permute-start(bf16[64,1024]{1,0:T(8,128)(2,1)} %bitcast.229), channel_id=1, source_target_pairs={{0,16},{2,18},{4,20},{6,22},{8,24},{10,26},{12,28},{14,30},{16,0},... | collective-permute-start | bytes 393224 | tf_op jit(solution)/shard_map/ppermute | solution.py:39
  84.6 50.1 %collective-permute-start.11 = (bf16[4,64,768]{2,1,0:T(8,128)(2,1)}, bf16[4,64,768]{2,1,0:T(8,128)(2,1)S(1)}, u32[]{:S(2)}, u32[]{:S(2)}) collective-permute-start(bf16[4,64,768]{2,1,0:T(8,128)(2,1)} %get-tuple-element.91.refs_2_), channel_id=1, source_target_pairs={{0,4},{2,6},{4,0},{6,2},{8,12},{10,14},{12,8},{14,10},{16,20},{18,... | collective-permute-start | bytes 1179656 | tf_op jit(solution)/shard_map/ppermute | solution.py:34
  86.2 46.0 %collective-permute-start.16 = (bf16[64,1024]{1,0:T(8,128)(2,1)}, bf16[64,1024]{1,0:T(8,128)(2,1)S(1)}, u32[]{:S(2)}, u32[]{:S(2)}) collective-permute-start(bf16[64,1024]{1,0:T(8,128)(2,1)} %bitcast.230), channel_id=1, source_target_pairs={{0,8},{2,10},{4,12},{6,14},{8,16},{10,18},{12,20},{14,22},{16,24},... | collective-permute-start | bytes 393224 | tf_op jit(solution)/shard_map/ppermute | solution.py:39
  87.1 47.6 %collective-permute-start.10 = (bf16[4,64,640]{2,1,0:T(8,128)(2,1)}, bf16[4,64,640]{2,1,0:T(8,128)(2,1)}, u32[]{:S(2)}, u32[]{:S(2)}) collective-permute-start(bf16[4,64,640]{2,1,0:T(8,128)(2,1)} %get-tuple-element.90.refs_0_), channel_id=1, source_target_pairs={{0,2},{2,0},{4,6},{6,4},{8,10},{10,8},{12,14},{14,12},{16,18},{18,... | collective-permute-start | bytes 983048 | tf_op jit(solution)/shard_map/ppermute | solution.py:34
  122.2 80.3 %collective-permute-start.14 = (bf16[4,2,64,512]{3,2,1,0:T(8,128)(2,1)}, bf16[4,2,64,512]{3,2,1,0:T(8,128)(2,1)S(1)}, u32[]{:S(2)}, u32[]{:S(2)}) collective-permute-start(bf16[4,2,64,512]{3,2,1,0:T(8,128)(2,1)} %get-tuple-element.97.refs_0_), channel_id=1, source_target_pairs={{0,4},{2,6},{4,0},{6,2},{8,12},{10,14},{12,8},{14,10},{16,20},{18,... | collective-permute-start | bytes 1572872 | tf_op jit(solution)/shard_map/ppermute | solution.py:34
  132.8 72.6 %collective-permute-start.15 = (bf16[4,2,64,512]{3,2,1,0:T(8,128)(2,1)}, bf16[4,2,64,512]{3,2,1,0:T(8,128)(2,1)S(1)}, u32[]{:S(2)}, u32[]{:S(2)}) collective-permute-start(bf16[4,2,64,512]{3,2,1,0:T(8,128)(2,1)} %get-tuple-element.98.refs_2_), channel_id=1, source_target_pairs={{0,2},{2,0},{4,6},{6,4},{8,10},{10,8},{12,14},{14,12},{16,18},{18,... | collective-permute-start | bytes 1572872 | tf_op jit(solution)/shard_map/ppermute | solution.py:34
  152.5 119.1 %collective-permute-start.19 = (bf16[4,64,512]{2,1,0:T(8,128)(2,1)}, bf16[4,64,512]{2,1,0:T(8,128)(2,1)}, u32[]{:S(2)}, u32[]{:S(2)}) collective-permute-start(bf16[4,64,512]{2,1,0:T(8,128)(2,1)} %get-tuple-element.109.refs_0_), channel_id=1, source_target_pairs={{0,2},{2,0},{4,6},{6,4},{8,10},{10,8},{12,14},{14,12},{16,18},{18,... | collective-permute-start | bytes 786440 | tf_op jit(solution)/shard_map/ppermute | solution.py:34
  154.0 117.6 %collective-permute-start.20 = (bf16[4,64,512]{2,1,0:T(8,128)(2,1)}, bf16[4,64,512]{2,1,0:T(8,128)(2,1)}, u32[]{:S(2)}, u32[]{:S(2)}) collective-permute-start(bf16[4,64,512]{2,1,0:T(8,128)(2,1)} %get-tuple-element.110.refs_2_), channel_id=1, source_target_pairs={{0,4},{2,6},{4,0},{6,2},{8,12},{10,14},{12,8},{14,10},{16,20},{18,... | collective-permute-start | bytes 786440 | tf_op jit(solution)/shard_map/ppermute | solution.py:34
  202.5 175.3 %collective-permute-start.13 = (bf16[4,2,64,768]{3,2,1,0:T(8,128)(2,1)}, bf16[4,2,64,768]{3,2,1,0:T(8,128)(2,1)}, u32[]{:S(2)}, u32[]{:S(2)}) collective-permute-start(bf16[4,2,64,768]{3,2,1,0:T(8,128)(2,1)} %get-tuple-element.93.refs_2_), channel_id=1, source_target_pairs={{0,2},{2,0},{4,6},{6,4},{8,10},{10,8},{12,14},{14,12},{16,18},{18,... | collective-permute-start | bytes 2359304 | tf_op jit(solution)/shard_map/ppermute | solution.py:34
  205.4 172.4 %collective-permute-start.12 = (bf16[4,2,64,640]{3,2,1,0:T(8,128)(2,1)}, bf16[4,2,64,640]{3,2,1,0:T(8,128)(2,1)}, u32[]{:S(2)}, u32[]{:S(2)}) collective-permute-start(bf16[4,2,64,640]{3,2,1,0:T(8,128)(2,1)} %get-tuple-element.92.refs_0_), channel_id=1, source_target_pairs={{0,4},{2,6},{4,0},{6,2},{8,12},{10,14},{12,8},{14,10},{16,20},{18,... | collective-permute-start | bytes 1966088 | tf_op jit(solution)/shard_map/ppermute | solution.py:34
  305.3 177.1 %collective-permute-start.21 = (bf16[4,2,64,512]{3,2,1,0:T(8,128)(2,1)}, bf16[4,2,64,512]{3,2,1,0:T(8,128)(2,1)}, u32[]{:S(2)}, u32[]{:S(2)}) collective-permute-start(bf16[4,2,64,512]{3,2,1,0:T(8,128)(2,1)} %get-tuple-element.111.refs_0_), channel_id=1, source_target_pairs={{0,4},{2,6},{4,0},{6,2},{8,12},{10,14},{12,8},{14,10},{16,20},{18,... | collective-permute-start | bytes 1572872 | tf_op jit(solution)/shard_map/ppermute | solution.py:34
  306.6 175.8 %collective-permute-start.22 = (bf16[4,2,64,512]{3,2,1,0:T(8,128)(2,1)}, bf16[4,2,64,512]{3,2,1,0:T(8,128)(2,1)}, u32[]{:S(2)}, u32[]{:S(2)}) collective-permute-start(bf16[4,2,64,512]{3,2,1,0:T(8,128)(2,1)} %get-tuple-element.112.refs_2_), channel_id=1, source_target_pairs={{0,2},{2,0},{4,6},{6,4},{8,10},{10,8},{12,14},{14,12},{16,18},{18,... | collective-permute-start | bytes 1572872 | tf_op jit(solution)/shard_map/ppermute | solution.py:34
  622.5 17.8 %collective-permute-start.26 = (bf16[512,640]{1,0:T(8,128)(2,1)}, bf16[512,640]{1,0:T(8,128)(2,1)S(1)}, u32[]{:S(2)}, u32[]{:S(2)}) collective-permute-start(bf16[512,640]{1,0:T(8,128)(2,1)} %get-tuple-element.134), channel_id=1, source_target_pairs={{0,4},{2,6},{4,0},{6,2},{8,12},{10,14},{12,8},{14,10},{16,20},{18,... | collective-permute-start | bytes 1966088 | tf_op jit(solution)/shard_map/ppermute | solution.py:34
  623.4 20.6 %collective-permute-start.28 = (bf16[512,768]{1,0:T(8,128)(2,1)}, bf16[512,768]{1,0:T(8,128)(2,1)S(1)}, u32[]{:S(2)}, u32[]{:S(2)}) collective-permute-start(bf16[512,768]{1,0:T(8,128)(2,1)} %get-tuple-element.136), channel_id=1, source_target_pairs={{0,2},{2,0},{4,6},{6,4},{8,10},{10,8},{12,14},{14,12},{16,18},{18,... | collective-permute-start | bytes 2359304 | tf_op jit(solution)/shard_map/ppermute | solution.py:34
  623.9 49.8 %collective-permute-start.34 = (bf16[512,1024]{1,0:T(8,128)(2,1)}, bf16[512,1024]{1,0:T(8,128)(2,1)S(1)}, u32[]{:S(2)}, u32[]{:S(2)}) collective-permute-start(bf16[512,1024]{1,0:T(8,128)(2,1)} %get-tuple-element.138), channel_id=1, source_target_pairs={{0,2},{2,0},{4,6},{6,4},{8,10},{10,8},{12,14},{14,12},{16,18},{18,... | collective-permute-start | bytes 3145736 | tf_op jit(solution)/shard_map/ppermute | solution.py:34
  625.4 50.5 %collective-permute-start.40 = (bf16[512,1024]{1,0:T(8,128)(2,1)}, bf16[512,1024]{1,0:T(8,128)(2,1)S(1)}, u32[]{:S(2)}, u32[]{:S(2)}) collective-permute-start(bf16[512,1024]{1,0:T(8,128)(2,1)} %get-tuple-element.143), channel_id=1, source_target_pairs={{0,4},{2,6},{4,0},{6,2},{8,12},{10,14},{12,8},{14,10},{16,20},{18,... | collective-permute-start | bytes 3145736 | tf_op jit(solution)/shard_map/ppermute | solution.py:34
  627.9 57.1 %collective-permute-start.24 = (f32[256,1024]{1,0:T(8,128)S(1)}, f32[256,1024]{1,0:T(8,128)S(1)}, u32[]{:S(2)}, u32[]{:S(2)}) collective-permute-start(f32[256,1024]{1,0:T(8,128)S(1)} %pad_maximum_fusion.3), channel_id=1, source_target_pairs={{0,1},{1,0},{2,3},{3,2},{4,5},{5,4},{6,7},{7,6},{8,9},{9,8},{10,11... | collective-permute-start | bytes 3145736 | tf_op jit(solution)/shard_map/ppermute | solution.py:44
  640.4 37.4 %collective-permute-start.25 = (f32[256,1024]{1,0:T(8,128)S(1)}, f32[256,1024]{1,0:T(8,128)S(1)}, u32[]{:S(2)}, u32[]{:S(2)}) collective-permute-start(f32[256,1024]{1,0:T(8,128)S(1)} %copy-done.54), channel_id=1, source_target_pairs={{0,1},{1,0},{2,3},{3,2},{4,5},{5,4},{6,7},{7,6},{8,9},{9,8},{10,11... | collective-permute-start | bytes 3145736 | tf_op jit(solution)/shard_map/ppermute | solution.py:44
  644.0 28.4 %collective-permute-start.27 = (bf16[4,64,640]{2,1,0:T(8,128)(2,1)S(1)}, bf16[4,64,640]{2,1,0:T(8,128)(2,1)S(1)}, u32[]{:S(2)}, u32[]{:S(2)}) collective-permute-start(bf16[4,64,640]{2,1,0:T(8,128)(2,1)S(1)} %fusion.20), channel_id=1, source_target_pairs={{0,2},{2,0},{4,6},{6,4},{8,10},{10,8},{12,14},{14,12},{16,18},{18,... | collective-permute-start | bytes 983048 | tf_op jit(solution)/shard_map/ppermute | solution.py:34
  675.1 56.6 %collective-permute-start.35 = (bf16[4,64,1024]{2,1,0:T(8,128)(2,1)}, bf16[4,64,1024]{2,1,0:T(8,128)(2,1)}, u32[]{:S(2)}, u32[]{:S(2)}) collective-permute-start(bf16[4,64,1024]{2,1,0:T(8,128)(2,1)} %fusion.7), channel_id=1, source_target_pairs={{0,4},{2,6},{4,0},{6,2},{8,12},{10,14},{12,8},{14,10},{16,20},{18,... | collective-permute-start | bytes 1572872 | tf_op jit(solution)/shard_map/ppermute | solution.py:34
  677.3 60.1 %collective-permute-start.41 = (bf16[4,64,1024]{2,1,0:T(8,128)(2,1)}, bf16[4,64,1024]{2,1,0:T(8,128)(2,1)}, u32[]{:S(2)}, u32[]{:S(2)}) collective-permute-start(bf16[4,64,1024]{2,1,0:T(8,128)(2,1)} %fusion.8), channel_id=1, source_target_pairs={{0,2},{2,0},{4,6},{6,4},{8,10},{10,8},{12,14},{14,12},{16,18},{18,... | collective-permute-start | bytes 1572872 | tf_op jit(solution)/shard_map/ppermute | solution.py:34
  696.2 33.4 %collective-permute-start.30 = (bf16[64,1408]{1,0:T(8,128)(2,1)}, bf16[64,1408]{1,0:T(8,128)(2,1)}, u32[]{:S(2)}, u32[]{:S(2)}) collective-permute-start(bf16[64,1408]{1,0:T(8,128)(2,1)} %get-tuple-element.165), channel_id=1, source_target_pairs={{0,8},{2,10},{4,12},{6,14},{8,16},{10,18},{12,20},{14,22},{16,24},... | collective-permute-start | bytes 540680 | tf_op jit(solution)/shard_map/ppermute | solution.py:39
  698.1 31.4 %collective-permute-start.32 = (bf16[64,1408]{1,0:T(8,128)(2,1)}, bf16[64,1408]{1,0:T(8,128)(2,1)}, u32[]{:S(2)}, u32[]{:S(2)}) collective-permute-start(bf16[64,1408]{1,0:T(8,128)(2,1)} %get-tuple-element.166), channel_id=1, source_target_pairs={{0,24},{2,26},{4,28},{6,30},{8,0},{10,2},{12,4},{14,6},{16,8},{18,... | collective-permute-start | bytes 540680 | tf_op jit(solution)/shard_map/ppermute | solution.py:39
  703.0 26.6 %collective-permute-start.31 = (bf16[64,1408]{1,0:T(8,128)(2,1)}, bf16[64,1408]{1,0:T(8,128)(2,1)}, u32[]{:S(2)}, u32[]{:S(2)}) collective-permute-start(bf16[64,1408]{1,0:T(8,128)(2,1)} %get-tuple-element.167), channel_id=1, source_target_pairs={{0,16},{2,18},{4,20},{6,22},{8,24},{10,26},{12,28},{14,30},{16,0},... | collective-permute-start | bytes 540680 | tf_op jit(solution)/shard_map/ppermute | solution.py:39
  731.4 27.6 %collective-permute-start.33 = (f32[32,1408]{1,0:T(8,128)S(1)}, f32[32,1408]{1,0:T(8,128)S(1)}, u32[]{:S(2)}, u32[]{:S(2)}) collective-permute-start(f32[32,1408]{1,0:T(8,128)S(1)} %get-tuple-element.174), channel_id=1, source_target_pairs={{0,1},{1,0},{2,3},{3,2},{4,5},{5,4},{6,7},{7,6},{8,9},{9,8},{10,11... | collective-permute-start | bytes 540680 | tf_op jit(solution)/shard_map/ppermute | solution.py:44
  738.7 17.7 %collective-permute-start.44 = (bf16[64,1024]{1,0:T(8,128)(2,1)S(1)}, bf16[64,1024]{1,0:T(8,128)(2,1)S(1)}, u32[]{:S(2)}, u32[]{:S(2)}) collective-permute-start(bf16[64,1024]{1,0:T(8,128)(2,1)S(1)} %get-tuple-element.168), channel_id=1, source_target_pairs={{0,24},{2,26},{4,28},{6,30},{8,0},{10,2},{12,4},{14,6},{16,8},{18,... | collective-permute-start | bytes 393224 | tf_op jit(solution)/shard_map/ppermute | solution.py:39
  (74 other events, 1298.4 us)
where the time goes:
time: 769 us; the launch traced here: 762 us
  Pallas kernels  542 us (70%)
  waiting for transfers between devices  72.9 us (9%)
  starting transfers between devices  56.9 us (7%)
  local copies, waits for them, and re-layouts  45.8 us (6%)
  other arithmetic  30 us (4%)
  matrix products  12.2 us (2%)
    pallas_call x11, Pallas kernels, place(): pl.pallas_call(functools.partial(place_kernel, moves=moves, inputs=len(pi...  467 us
    ppermute x24, waiting for transfers between devices, swapped(): lax.ppermute(x, 'dp', [(i, i ^ bit) for i in range(lax.axis_size('dp'))])  53.4 us
    ppermute x18, starting transfers between devices, column_shift(): lax.ppermute(x, 'dp', [(i, (i + PLANE * steps) % size) for i in range(siz...  31.7 us
    pallas_call x2, Pallas kernels, mix_backward(): pl.pallas_call(functools.partial(scan_backward, lead=heads * part, final=...  28.7 us
    ppermute x24, starting transfers between devices, swapped(): lax.ppermute(x, 'dp', [(i, i ^ bit) for i in range(lax.axis_size('dp'))])  24.5 us
    pallas_call x4, Pallas kernels, halves(): pl.pallas_call(functools.partial(halves_kernel, parts=len(rights), tall=t...  18.7 us
    ppermute x18, waiting for transfers between devices, column_shift(): lax.ppermute(x, 'dp', [(i, (i + PLANE * steps) % size) for i in range(siz...  18.5 us
    pallas_call x2, Pallas kernels, mix_forward(): pl.pallas_call(functools.partial(scan_forward, lead=heads * part), grid=(...  16.9 us
  transfers between devices with their start and end apart: 50, of which 13 were waited for; matrix products, arithmetic and copies ran while one was open for 9% of the time, Pallas kernels for 54%

commit v1 on v0

--- a/solution.py
+++ b/solution.py
@@ -54,33 +54,35 @@
 def dp_sum(x):
     size = lax.axis_size("dp")
     if size & (size - 1):
-        return lax.psum(x, "dp")
-    bit = size // 2
-    while bit:
+        return lax.psum(x, "dp"), x
+    bit = 1
+    gate = x
+    while bit < size:
         x = x + swapped(x, bit)
-        bit //= 2
-    return x
+        gate = x if bit < PLANE else gate
+        bit *= 2
+    return x, gate
 
 
 def place_kernel(at_ref, *refs, moves, inputs):
-    ins, outs, sems = refs[:inputs], refs[inputs:-1], refs[-1]
-    copies = []
-    for n, (source, columns, target, where) in enumerate(moves):
-        src = ins[source] if columns is None else ins[source].at[..., slice(*columns)]
-        copies.append(pltpu.make_async_copy(src, outs[target].at[where(at_ref)], sems.at[n]))
-    for copy in copies:
-        copy.start()
-    for copy in copies:
-        copy.wait()
-
-
-def place(at, pieces, shapes, moves):
+    ins, outs = refs[:inputs], refs[inputs:]
+    for source, columns, target, where in moves:
+        cols = slice(None) if columns is None else slice(*columns)
+        outs[target][where(at_ref)] = ins[source][..., cols]
+
+
+def place(at, pieces, shapes, moves, stepped=False):
+    def spec(shape):
+        if not stepped:
+            return full()
+        return pl.BlockSpec((1,) + shape[1:], lambda i: (i,) + (0,) * (len(shape) - 1))
+
     return pl.pallas_call(
         functools.partial(place_kernel, moves=moves, inputs=len(pieces)),
-        in_specs=[scalar()] + [pl.BlockSpec(memory_space=pl.ANY)] * len(pieces),
-        out_specs=[pl.BlockSpec(memory_space=pl.ANY)] * len(shapes),
+        grid=(pieces[0].shape[0],) if stepped else (),
+        in_specs=[scalar()] + [spec(v.shape) for v in pieces],
+        out_specs=[spec(shape) for shape in shapes],
         out_shape=[jax.ShapeDtypeStruct(shape, pieces[0].dtype) for shape in shapes],
-        scratch_shapes=[pltpu.SemaphoreType.DMA((len(moves),))],
     )(at, *pieces)
 
 
@@ -111,6 +113,7 @@
             (2, None, 1, lambda ref: (every, ref[1])),
             (3, None, 1, lambda ref: (every, 1 - ref[1])),
         ],
+        True,
     )
     left_far, right_far = swapped(left, 2), swapped(right, 1)
     left, right = place(
@@ -123,6 +126,7 @@
             (2, None, 1, lambda ref: (every, every, ref[2])),
             (3, None, 1, lambda ref: (every, every, 1 - ref[2])),
         ],
+        True,
     )
     return left.reshape(-1, cut), right.reshape(-1, rest), later
 
@@ -645,6 +649,23 @@
     out_ref[:, step_at : step_at + heads] = total
 
 
+def own_params(at_ref, rows_ref, heads_ref, own_ref, own_heads_ref):
+    even = at_ref[0] == 0
+    lane = lax.broadcasted_iota(jnp.int32, (1, 128), 1)
+    for at in range(0, own_ref.shape[1], 128):
+        a, b = rows_ref[:, 2 * at : 2 * at + 128], rows_ref[:, 2 * at + 128 : 2 * at + 256]
+        low = jnp.where(lane < HEAD_DIM, a, pltpu.roll(b, HEAD_DIM, 1))
+        high = jnp.where(lane < HEAD_DIM, pltpu.roll(a, HEAD_DIM, 1), b)
+        own_ref[:, at : at + 128] = jnp.where(even, low, high)
+    heads = heads_ref.shape[1]
+    row = lax.broadcasted_iota(jnp.int32, (heads, 128), 0)
+    col = lax.broadcasted_iota(jnp.int32, (heads, 128), 1)
+    choice = jnp.where((row == 2 * col + at_ref[0]) & (col < heads // 2), 1.0, 0.0)
+    own_heads_ref[...] = lax.dot_general(
+        heads_ref[...], choice, (((1,), (0,)), ((), ())), precision=PRECISE, preferred_element_type=jnp.float32
+    )
+
+
 def scalar():
     return pl.BlockSpec(memory_space=pltpu.SMEM)
 
@@ -811,35 +832,48 @@
         out_all = split.own(lax.all_gather(out_weight, ("dp", "seq"), axis=0, tiled=True).T).T
         out_left, out_right = out_all[:, : d_model // 2], out_all[:, d_model // 2 :]
 
-    own_bias = split.own(step_bias)
-    rates = -jnp.exp(split.own(log_rate))
-    own_gain = split.own(gate_gain)
-    conv_x = split.own(conv_weight[:, :D_INNER])
-    params = jnp.concatenate(
+    rows = jnp.concatenate(
         [
-            conv_x,
-            split.own(conv_bias[:D_INNER])[None],
-            jnp.repeat(split.own(skip_weight), HEAD_DIM)[None],
-            own_gain[None],
-            jnp.zeros((1, inner), jnp.float32),
+            conv_weight[:, :D_INNER],
+            conv_bias[None, :D_INNER],
+            jnp.repeat(skip_weight, HEAD_DIM)[None],
+            gate_gain[None],
+            jnp.zeros((1, D_INNER), jnp.float32),
         ],
         axis=0,
     )
+    head_pair = jnp.concatenate([step_bias[None], log_rate[None], jnp.zeros((6, HEADS), jnp.float32)], axis=0)
+    if split.staged:
+        params, head_pair = pl.pallas_call(
+            own_params,
+            in_specs=[scalar(), full(), full()],
+            out_specs=[full(), full()],
+            out_shape=[
+                jax.ShapeDtypeStruct((8, inner), jnp.float32),
+                jax.ShapeDtypeStruct((8, lanes), jnp.float32),
+            ],
+            name="own",
+        )(at.reshape(1), rows, head_pair)
+    else:
+        params = split.own(rows)
+        head_pair = jnp.pad(split.own(head_pair), ((0, 0), (0, lanes - heads)))
+    own_gain = params[CONVK + 2]
+    own_bias = head_pair[0:1]
+    all_rates = jnp.where(jnp.arange(lanes)[None, :] < heads, -jnp.exp(head_pair[1:2]), 0.0)
     tri = (jnp.arange(GROUP)[:, None] >= jnp.arange(GROUP)[None, :]).astype(jnp.float32)
 
+    bc_params = jnp.concatenate(
+        [conv_weight[:, D_INNER:], conv_bias[None, D_INNER:], jnp.zeros((3, 2 * STATE), jnp.float32)], axis=0
+    )
     step_raw = dot(normed, x_first[:, half:], ((1,), (0,)))
-    step_in = step_raw + jnp.pad(own_bias, (0, lanes - heads))[None, :]
-    all_rates = jnp.pad(rates, (0, lanes - heads))[None, :]
+    step_in = step_raw + own_bias
     deltas = jax.nn.softplus(step_in)
     cum = jnp.einsum(
         "ts,gsh->gth", tri, (deltas * all_rates).reshape(groups, GROUP, lanes), precision=PRECISE
     ).reshape(count, lanes)
     cum_t = cum.T
     bc_in = dot(normed, gate_first[:, half:], ((1,), (0,))).astype(bf)
-    bc_params = jnp.concatenate(
-        [conv_weight[:, D_INNER:], conv_bias[None, D_INNER:], jnp.zeros((3, 2 * STATE), jnp.float32)], axis=0
-    )
-    bc = conv_act(bc_in.astype(jnp.float32), conv_weight[:, D_INNER:], conv_bias[D_INNER:])
+    bc = conv_act(bc_in.astype(jnp.float32), bc_params[:CONVK], bc_params[CONVK])
 
     pulled = dot(top_left, out_left, ((1,), (1,))) + dot(top_right, out_right, ((1,), (1,)))
     saved = []
@@ -861,14 +895,15 @@
     )
     if split.staged:
         out_halves = halves(normed_out, (top_left, top_right), 2)
-        out_parts = column_sum(*plane_sum(*out_halves, 2))
+        out_column, _ = plane_sum(*out_halves, 2)
 
     gx1, ggate1, *carried, gpar1 = mix_backward(
         1, half_heads, *saved[1][:4], pulled, norms, bc, deltas, cum, cum_t, params
     )
     if split.staged:
         second_halves = halves(normed, (gx1, ggate1), 1)
-        second_parts = column_sum(*plane_sum(*second_halves, 1))
+        second_column, gate = plane_sum(*second_halves, 1)
+        second_parts = column_sum(jnp.concatenate([out_column, second_column], axis=-1), gate)
     gx0, ggate0, _, _, _, gpar0, gstep, gbc, gheads, gbc_par = mix_backward(
         0, half_heads, *saved[0][:4], pulled, norms, bc, deltas, cum, cum_t, params,
         *carried, bc_in, step_in, jnp.broadcast_to(all_rates, (8, lanes)), bc_params,
@@ -904,7 +939,7 @@
     grad_stream, grad_norm_gain = norm_back(grad_normed)
 
     small = (gpar0, gpar1, gbc_par, gheads, grad_norm_gain)
-    packed = dp_sum(jnp.concatenate([v.reshape(-1, 128) for v in small]))
+    packed, packed_gate = dp_sum(jnp.concatenate([v.reshape(-1, 128) for v in small]))
     other_packed = None
     if split.staged:
         other_packed = seq_shift(packed, 1)
@@ -944,10 +979,10 @@
     )
 
     if split.staged:
-        out_share = arrived_sum(out_parts, gate)
+        both_share = arrived_sum(second_parts, gate)
+        out_share = both_share[:, :d_model]
         pairs = []
-        for parts, after in ((first_parts, None), (second_parts, gate)):
-            share = arrived_sum(parts, after)
+        for share in (arrived_sum(first_parts, packed_gate), both_share[:, d_model:]):
             pair = share.reshape(peers, -1, share.shape[-1])
             pairs += [pick(pair, at, 0), seq_shift(pick(pair, 1 - at, 0), 1)]
         in_share = zip_columns(at, *pairs, half)

time: 769 us -> 347 us (0.45)
  Pallas kernels: 542 us -> 110 us
  waiting for transfers between devices: 72.9 us -> 106 us
  local copies, waits for them, and re-layouts: 45.8 us -> 32.5 us
  starting transfers between devices: 56.9 us -> 48.5 us
    pallas_call x11, Pallas kernels: 467 us -> 33.3 us  [place(): pl.pallas_call(functools.partial(place_kernel, moves=moves, inputs=len(pi...]
    ppermute x24, waiting for transfers between devices: 53.4 us -> 73.9 us  [swapped(): lax.ppermute(x, 'dp', [(i, i ^ bit) for i in range(lax.axis_size('dp'))])]
    ppermute x18 -> x15, waiting for transfers between devices: 18.5 us -> 31.2 us  [column_shift(): lax.ppermute(x, 'dp', [(i, (i + PLANE * steps) % size) for i in range(siz...]
    ppermute x18 -> x15, starting transfers between devices: 31.7 us -> 25.3 us  [column_shift(): lax.ppermute(x, 'dp', [(i, (i + PLANE * steps) % size) for i in range(siz...]
  transfers between devices with their start and end apart: 50 -> 47, of which waited for: 13 -> 17; matrix products, arithmetic and copies ran while one was open for 9% -> 17% of each run, Pallas kernels for 54% -> 12%
where the time goes in v1:
time: 347 us; the launch traced here: 341 us
  Pallas kernels  110 us (32%)
  waiting for transfers between devices  106 us (31%)
  starting transfers between devices  48.5 us (14%)
  local copies, waits for them, and re-layouts  32.5 us (9%)
  other arithmetic  30.6 us (9%)
  matrix products  12.1 us (3%)
    ppermute x24, waiting for transfers between devices, swapped(): lax.ppermute(x, 'dp', [(i, i ^ bit) for i in range(lax.axis_size('dp'))])  73.9 us
    pallas_call x11, Pallas kernels, place(): pl.pallas_call(functools.partial(place_kernel, moves=moves, inputs=len(pi...  33.3 us
    ppermute x15, waiting for transfers between devices, column_shift(): lax.ppermute(x, 'dp', [(i, (i + PLANE * steps) % size) for i in range(siz...  31.2 us
    pallas_call x2, Pallas kernels, mix_backward(): pl.pallas_call(functools.partial(scan_backward, lead=heads * part, final=...  28.6 us
    ppermute x15, starting transfers between devices, column_shift(): lax.ppermute(x, 'dp', [(i, (i + PLANE * steps) % size) for i in range(siz...  25.3 us
    ppermute x24, starting transfers between devices, swapped(): lax.ppermute(x, 'dp', [(i, i ^ bit) for i in range(lax.axis_size('dp'))])  23 us
    pallas_call x4, Pallas kernels, halves(): pl.pallas_call(functools.partial(halves_kernel, parts=len(rights), tall=t...  18.7 us
    pallas_call x2, Pallas kernels, mix_forward(): pl.pallas_call(functools.partial(scan_forward, lead=heads * part), grid=(...  16.6 us
  transfers between devices with their start and end apart: 47, of which 17 were waited for; matrix products, arithmetic and copies ran while one was open for 17% of the time, Pallas kernels for 12%

profile of v1, /device:TPU:14, one launch (start us, length us, event | category | flops | bytes accessed | tf_op | source)
XLA Modules:
  0.0 341.5 jit_solution(7795488786025457139)
XLA Ops:
  11.4 3.3 collective-permute-done.5.refs_1_
  21.4 3.8 %collective-permute-start.3 = (bf16[64,1408]{1,0:T(8,128)(2,1)}, bf16[64,1408]{1,0:T(8,128)(2,1)}, u32[]{:S(2)}, u32[]{:S(2)}) collective-permute-start(bf16[64,1408]{1,0:T(8,128)(2,1)} %bitcast.222), channel_id=1, source_target_pairs={{0,16},{2,18},{4,20},{6,22},{8,24},{10,26},{12,28},{14,30},{16,0},... | collective-permute-start | bytes 540680 | tf_op jit(solution)/shard_map/ppermute | solution.py:39
  26.3 4.7 %collective-permute-done.4.refs_3_ = bf16[64,1408]{1,0:T(8,128)(2,1)} collective-permute-done((bf16[64,1408]{1,0:T(8,128)(2,1)}, bf16[64,1408]{1,0:T(8,128)(2,1)}, u32[]{:S(2)}, u32[]{:S(2)}) %collective-permute-start.4) | collective-permute-done | bytes 180256 | tf_op jit(solution)/shard_map/ppermute | solution.py:39
  31.0 3.9 %collective-permute-done.3.refs_2_ = bf16[64,1408]{1,0:T(8,128)(2,1)} collective-permute-done((bf16[64,1408]{1,0:T(8,128)(2,1)}, bf16[64,1408]{1,0:T(8,128)(2,1)}, u32[]{:S(2)}, u32[]{:S(2)}) %collective-permute-start.3) | collective-permute-done | bytes 180256 | tf_op jit(solution)/shard_map/ppermute | solution.py:39
  34.9 6.8 %collective-permute-start.18 = (bf16[64,1024]{1,0:T(8,128)(2,1)}, bf16[64,1024]{1,0:T(8,128)(2,1)S(1)}, u32[]{:S(2)}, u32[]{:S(2)}) collective-permute-start(bf16[64,1024]{1,0:T(8,128)(2,1)} %bitcast.28.refs_0_), channel_id=1, source_target_pairs={{0,24},{2,26},{4,28},{6,30},{8,0},{10,2},{12,4},{14,6},{16,8},{18,... | collective-permute-start | bytes 393224 | tf_op jit(solution)/shard_map/ppermute | solution.py:39
  49.1 3.4 shard_map.200
  59.2 5.5 %collective-permute-done.11.refs_3_ = bf16[4,64,768]{2,1,0:T(8,128)(2,1)S(1)} collective-permute-done((bf16[4,64,768]{2,1,0:T(8,128)(2,1)}, bf16[4,64,768]{2,1,0:T(8,128)(2,1)S(1)}, u32[]{:S(2)}, u32[]{:S(2)}) %collective-permute-start.11) | collective-permute-done | bytes 393248 | tf_op jit(solution)/shard_map/ppermute | solution.py:34
  70.3 3.6 %shard_map.198 = (bf16[4,2,64,640]{3,2,1,0:T(8,128)(2,1)}, bf16[4,2,64,768]{3,2,1,0:T(8,128)(2,1)}) custom-call(s32[3]{0:T(128)} %pad_add_fusion.at_ref, bf16[4,64,640]{2,1,0:T(8,128)(2,1)} %get-tuple-element.92.refs_0_, bf16[4,64,640]{2,1,0:T(8,128)(2,1)} %collective-permute-done.10.refs_1_, bf16[4,64,768]{2,1,0:T(8,128)(2,1)} %get-tuple-element.93.refs_2_, ...), custom_call_target="tpu_custom_call" | custom-call | tf_op jit(solution)/shard_map/pallas_call | solution.py:80
  78.9 3.9 %shard_map.201 = (bf16[4,2,2,64,512]{4,3,2,1,0:T(8,128)(2,1)}, bf16[4,2,2,64,512]{4,3,2,1,0:T(8,128)(2,1)}) custom-call(s32[3]{0:T(128)} %pad_add_fusion.at_ref, bf16[4,2,64,512]{3,2,1,0:T(8,128)(2,1)} %get-tuple-element.99.refs_0_, bf16[4,2,64,512]{3,2,1,0:T(8,128)(2,1)} %copy-done.22, bf16[4,2,64,512]{3,2,1,0:T(8,128)(2,1)} %get-tuple-element.100.refs_2_, ...), custom_call_target="tpu_custom_call" | custom-call | tf_op jit(solution)/shard_map/pallas_call | solution.py:80
  82.7 3.5 %shard_map.203 = (bf16[4,2,64,512]{3,2,1,0:T(8,128)(2,1)}, bf16[4,2,64,512]{3,2,1,0:T(8,128)(2,1)}) custom-call(s32[3]{0:T(128)} %pad_add_fusion.at_ref, bf16[4,64,512]{2,1,0:T(8,128)(2,1)} %get-tuple-element.113.refs_0_, bf16[4,64,512]{2,1,0:T(8,128)(2,1)} %collective-permute-done.19.refs_1_, bf16[4,64,512]{2,1,0:T(8,128)(2,1)} %get-tuple-element.114.refs_2_, ...), custom_call_target="tpu_custom_call" | custom-call | tf_op jit(solution)/shard_map/pallas_call | solution.py:80
  89.4 3.0 shard_map.194
  96.7 4.3 %shard_map.199 = (bf16[4,2,2,64,640]{4,3,2,1,0:T(8,128)(2,1)}, bf16[4,2,2,64,768]{4,3,2,1,0:T(8,128)(2,1)}) custom-call(s32[3]{0:T(128)} %pad_add_fusion.at_ref, bf16[4,2,64,640]{3,2,1,0:T(8,128)(2,1)} %get-tuple-element.94.refs_0_, bf16[4,2,64,640]{3,2,1,0:T(8,128)(2,1)} %collective-permute-done.12.refs_1_, ...), custom_call_target="tpu_custom_call" | custom-call | tf_op jit(solution)/shard_map/pallas_call | solution.py:80
  107.7 8.2 %scan.2 = (bf16[512,512]{1,0:T(8,128)(2,1)}, f32[512,512]{1,0:T(8,128)}, f32[512,512]{1,0:T(8,128)}, f32[2,128,512]{2,1,0:T(8,128)}, f32[512,256]{1,0:T(8,128)}) custom-call(bf16[512,1024]{1,0:T(8,128)(2,1)} %bitcast.175, bf16[1024,640]{1,0:T(8,128)(2,1)} %bitcast.188, bf16[1024,768]{1,0:T(8,128)(2,1)} %bitcast.184, ...), custom_call_target="tpu_custom_call" | custom-call | tf_op jit(solution)/shard_map/scan/pallas_call | solution.py:442
  116.0 3.9 %shard_map.204 = (bf16[4,2,2,64,512]{4,3,2,1,0:T(8,128)(2,1)}, bf16[4,2,2,64,512]{4,3,2,1,0:T(8,128)(2,1)}) custom-call(s32[3]{0:T(128)} %pad_add_fusion.at_ref, bf16[4,2,64,512]{3,2,1,0:T(8,128)(2,1)} %get-tuple-element.115.refs_0_, bf16[4,2,64,512]{3,2,1,0:T(8,128)(2,1)} %collective-permute-done.21.refs_1_, ...), custom_call_target="tpu_custom_call" | custom-call | tf_op jit(solution)/shard_map/pallas_call | solution.py:80
  119.8 8.4 %scan.3 = (bf16[512,512]{1,0:T(8,128)(2,1)}, f32[512,512]{1,0:T(8,128)}, f32[512,512]{1,0:T(8,128)}, f32[2,128,512]{2,1,0:T(8,128)}, f32[512,256]{1,0:T(8,128)}) custom-call(bf16[512,1024]{1,0:T(8,128)(2,1)} %bitcast.176, bf16[1024,512]{1,0:T(8,128)(2,1)} %bitcast.202, bf16[1024,512]{1,0:T(8,128)(2,1)} %bitcast.204, ...), custom_call_target="tpu_custom_call" | custom-call | tf_op jit(solution)/shard_map/scan/pallas_call | solution.py:442
  138.0 12.7 %unscan.2 = (bf16[512,512]{1,0:T(8,128)(2,1)}, bf16[512,512]{1,0:T(8,128)(2,1)}, f32[512,256]{1,0:T(8,128)}, f32[512,128]{1,0:T(8,128)}, f32[512,128]{1,0:T(8,128)}, /*index=5*/f32[8,512]{1,0:T(8,128)}) custom-call(bf16[512,512]{1,0:T(8,128)(2,1)} %get-tuple-element.124.x_ref, f32[512,512]{1,0:T(8,128)} %get-tuple-element.121.gate_ref, ...), custom_call_target="tpu_custom_call" | custom-call | tf_op jit(solution)/shard_map/unscan/pallas_call | solution.py:505
  151.3 15.9 %unscan.3 = (bf16[512,512]{1,0:T(8,128)(2,1)}, bf16[512,512]{1,0:T(8,128)(2,1)}, f32[512,256]{1,0:T(8,128)}, f32[512,128]{1,0:T(8,128)}, f32[512,128]{1,0:T(8,12...) custom-call(bf16[512,512]{1,0:T(8,128)(2,1)} %get-tuple-element.122., ...), custom_call_target="tpu_custom_call" | custom-call | tf_op jit(solution)/shard_map/unscan/pallas_call | solution.py:505
  168.7 4.8 %halves.7 = (bf16[512,1024]{1,0:T(8,128)(2,1)}, bf16[512,1024]{1,0:T(8,128)(2,1)}) custom-call(s32[1]{0:T(128)} %bitcast.45.at_ref, bf16[512,1024]{1,0:T(8,128)(2,1)} %bitcast.177, bf16[512,512]{1,0:T(8,128)(2,1)} %get-tuple-element.133.refs_4_.refs_1_, bf16[512,512]{1,0:T(8,128)(2,1)} %get-tuple-element.134.refs_5_.refs_2_), custom_call_target="tpu_custom_call" | custom-call | tf_op jit(solution)/shard_map/halves/pallas_call | solution.py:550
  173.5 4.5 %halves.5 = (bf16[512,768]{1,0:T(8,128)(2,1)}, bf16[512,768]{1,0:T(8,128)(2,1)}) custom-call(s32[1]{0:T(128)} %bitcast.45.at_ref, bf16[512,1024]{1,0:T(8,128)(2,1)} %bitcast.178, bf16[512,512]{1,0:T(8,128)(2,1)} %get-tuple-element.131.refs_2_.refs_1_, bf16[512,256]{1,0:T(8,128)(2,1)} %get-tuple-element.132.refs_3_.refs_2_), custom_call_target="tpu_custom_call" | custom-call | tf_op jit(solution)/shard_map/halves/pallas_call | solution.py:550
  178.1 7.1 %product.1 = (f32[256,1024]{1,0:T(8,128)}, f32[256,1024]{1,0:T(8,128)}) custom-call(s32[1]{0:T(128)} %bitcast.1.at_ref, bf16[512,512]{1,0:T(8,128)(2,1)} %get-tuple-element.129.refs_0_.refs_2_, bf16[512,128]{1,0:T(8,128)(2,1)} %get-tuple-element.130.refs_1_.refs_3_, bf16[512,512]{1,0:T(8,128)(2,1)} %get-tuple-element.131.refs_2_.refs_1_, ...), custom_call_target="tpu_custom_call" | custom-call | tf_op jit(solution)/shard_map/product/pallas_call | solution.py:577
  185.1 4.5 %halves.4 = (bf16[512,640]{1,0:T(8,128)(2,1)}, bf16[512,640]{1,0:T(8,128)(2,1)}) custom-call(s32[1]{0:T(128)} %bitcast.41.at_ref, bf16[512,1024]{1,0:T(8,128)(2,1)} %bitcast.179, bf16[512,1024]{1,0:T(8,128)(2,1)} %bitcast.180, bf16[512,512]{1,0:T(8,128)(2,1)} %get-tuple-element.129.refs_0_.refs_2_, bf16[512,128]{1,0:T(8,128)(2,1)} %get-tuple-element.130.refs_1_.refs_3_), custom_call_target="tpu_custom_call" | custom-call | tf_op jit(solution)/shard_map/halves/pallas_call | solution.py:550
  189.6 4.8 %halves.6 = (bf16[512,1024]{1,0:T(8,128)(2,1)}, bf16[512,1024]{1,0:T(8,128)(2,1)}) custom-call(s32[1]{0:T(128)} %bitcast.41.at_ref, bf16[512,1024]{1,0:T(8,128)(2,1)} %pad_maximum_fusion.2.refs_0_.refs_1_, bf16[512,1024]{1,0:T(8,128)(2,1)} %pad_maximum_fusion.2.refs_0_.refs_1_, bf16[512,512]{1,0:T(8,128)(2,1)} %bitcast.210, bf16[512,512]{1,0:T(8,128)(2,1)} %bitcast.209), custom_call_target="tpu_custom_call" | custom-call | tf_op jit(solution)/shard_map/halves/pallas_call | solution.py:550
  200.8 11.4 %collective-permute-done.26 = bf16[512,640]{1,0:T(8,128)(2,1)S(1)} collective-permute-done((bf16[512,640]{1,0:T(8,128)(2,1)}, bf16[512,640]{1,0:T(8,128)(2,1)S(1)}, u32[]{:S(2)}, u32[]{:S(2)}) %collective-permute-start.26) | collective-permute-done | bytes 655392 | tf_op jit(solution)/shard_map/ppermute | solution.py:34
  212.4 4.1 %collective-permute-done.28 = bf16[512,768]{1,0:T(8,128)(2,1)S(1)} collective-permute-done((bf16[512,768]{1,0:T(8,128)(2,1)}, bf16[512,768]{1,0:T(8,128)(2,1)S(1)}, u32[]{:S(2)}, u32[]{:S(2)}) %collective-permute-start.28) | collective-permute-done | bytes 786464 | tf_op jit(solution)/shard_map/ppermute | solution.py:34
  217.3 27.7 %collective-permute-done.27 = bf16[4,64,640]{2,1,0:T(8,128)(2,1)S(1)} collective-permute-done((bf16[4,64,640]{2,1,0:T(8,128)(2,1)S(1)}, bf16[4,64,640]{2,1,0:T(8,128)(2,1)S(1)}, u32[]{:S(2)}, u32[]{:S(2)}) %collective-permute-start.27) | collective-permute-done | bytes 327712 | tf_op jit(solution)/shard_map/ppermute | solution.py:34
  252.2 11.1 %collective-permute-done.33 = f32[96,128]{1,0:T(8,128)S(1)} collective-permute-done((f32[96,128]{1,0:T(8,128)S(1)}, f32[96,128]{1,0:T(8,128)S(1)}, u32[]{:S(2)}, u32[]{:S(2)}) %collective-permute-start.33) | collective-permute-done | bytes 49184 | tf_op jit(solution)/shard_map/ppermute | solution.py:34
  268.2 3.4 collective-permute-done.44
  276.1 6.6 %collective-permute-done.45 = f32[96,128]{1,0:T(8,128)S(1)} collective-permute-done((f32[96,128]{1,0:T(8,128)S(1)}, f32[96,128]{1,0:T(8,128)S(1)}, u32[]{:S(2)}, u32[]{:S(2)}) %collective-permute-start.45) | collective-permute-done | bytes 49184 | tf_op jit(solution)/shard_map/ppermute | solution.py:34
  308.2 3.4 collective-permute-start.41
  314.4 2.9 collective-permute-done.42
  317.3 10.8 %collective-permute-done.41 = bf16[64,2048]{1,0:T(8,128)(2,1)S(1)} collective-permute-done((bf16[64,2048]{1,0:T(8,128)(2,1)S(1)}, bf16[64,2048]{1,0:T(8,128)(2,1)S(1)}, u32[]{:S(2)}, u32[]{:S(2)}) %collective-permute-start.41) | collective-permute-done | bytes 262176 | tf_op jit(solution)/shard_map/ppermute | solution.py:39
  328.1 5.5 %collective-permute-done.40 = bf16[64,2048]{1,0:T(8,128)(2,1)S(1)} collective-permute-done((bf16[64,2048]{1,0:T(8,128)(2,1)S(1)}, bf16[64,2048]{1,0:T(8,128)(2,1)S(1)}, u32[]{:S(2)}, u32[]{:S(2)}) %collective-permute-start.40) | collective-permute-done | bytes 262176 | tf_op jit(solution)/shard_map/ppermute | solution.py:39
  (309 shorter events, 128.5 us)
Async XLA Ops:
  17.9 26.0 %collective-permute-start.8 = (bf16[4,64,512]{2,1,0:T(8,128)(2,1)}, bf16[4,64,512]{2,1,0:T(8,128)(2,1)S(1)}, u32[]{:S(2)}, u32[]{:S(2)}) collective-permute-start(bf16[4,64,512]{2,1,0:T(8,128)(2,1)} %get-tuple-element.87.refs_0_), channel_id=1, source_target_pairs={{0,2},{2,0},{4,6},{6,4},{8,10},{10,8},{12,14},{14,12},{16,18},{18,... | collective-permute-start | bytes 786440 | tf_op jit(solution)/shard_map/ppermute | solution.py:34
  18.5 27.0 %collective-permute-start.9 = (bf16[4,64,512]{2,1,0:T(8,128)(2,1)}, bf16[4,64,512]{2,1,0:T(8,128)(2,1)}, u32[]{:S(2)}, u32[]{:S(2)}) collective-permute-start(bf16[4,64,512]{2,1,0:T(8,128)(2,1)} %get-tuple-element.88.refs_2_), channel_id=1, source_target_pairs={{0,4},{2,6},{4,0},{6,2},{8,12},{10,14},{12,8},{14,10},{16,20},{18,... | collective-permute-start | bytes 786440 | tf_op jit(solution)/shard_map/ppermute | solution.py:34
  21.4 13.5 %collective-permute-start.3 = (bf16[64,1408]{1,0:T(8,128)(2,1)}, bf16[64,1408]{1,0:T(8,128)(2,1)}, u32[]{:S(2)}, u32[]{:S(2)}) collective-permute-start(bf16[64,1408]{1,0:T(8,128)(2,1)} %bitcast.222), channel_id=1, source_target_pairs={{0,16},{2,18},{4,20},{6,22},{8,24},{10,26},{12,28},{14,30},{16,0},... | collective-permute-start | bytes 540680 | tf_op jit(solution)/shard_map/ppermute | solution.py:39
  25.2 16.5 %collective-permute-start.2 = (bf16[64,1408]{1,0:T(8,128)(2,1)}, bf16[64,1408]{1,0:T(8,128)(2,1)}, u32[]{:S(2)}, u32[]{:S(2)}) collective-permute-start(bf16[64,1408]{1,0:T(8,128)(2,1)} %bitcast.223), channel_id=1, source_target_pairs={{0,8},{2,10},{4,12},{6,14},{8,16},{10,18},{12,20},{14,22},{16,24},... | collective-permute-start | bytes 540680 | tf_op jit(solution)/shard_map/ppermute | solution.py:39
  31.0 57.5 %collective-permute-start = (bf16[256,2048]{1,0:T(8,128)(2,1)S(1)}, bf16[256,2048]{1,0:T(8,128)(2,1)S(1)}, u32[]{:S(2)}, u32[]{:S(2)}) collective-permute-start(bf16[256,2048]{1,0:T(8,128)(2,1)S(1)} %pad_maximum_fusion.3.refs_0_), channel_id=1, source_target_pairs={{0,1},{1,0},{2,3},{3,2},{4,5},{5,4},{6,7},{7,6},{8,9},{9,8},{10,11... | collective-permute-start | bytes 3145736 | tf_op jit(solution)/shard_map/ppermute | solution.py:44
  34.9 17.5 %collective-permute-start.18 = (bf16[64,1024]{1,0:T(8,128)(2,1)}, bf16[64,1024]{1,0:T(8,128)(2,1)S(1)}, u32[]{:S(2)}, u32[]{:S(2)}) collective-permute-start(bf16[64,1024]{1,0:T(8,128)(2,1)} %bitcast.28.refs_0_), channel_id=1, source_target_pairs={{0,24},{2,26},{4,28},{6,30},{8,0},{10,2},{12,4},{14,6},{16,8},{18,... | collective-permute-start | bytes 393224 | tf_op jit(solution)/shard_map/ppermute | solution.py:39
  44.0 13.4 %collective-permute-start.16 = (bf16[64,1024]{1,0:T(8,128)(2,1)}, bf16[64,1024]{1,0:T(8,128)(2,1)S(1)}, u32[]{:S(2)}, u32[]{:S(2)}) collective-permute-start(bf16[64,1024]{1,0:T(8,128)(2,1)} %bitcast.28.refs_0_), channel_id=1, source_target_pairs={{0,8},{2,10},{4,12},{6,14},{8,16},{10,18},{12,20},{14,22},{16,24},... | collective-permute-start | bytes 393224 | tf_op jit(solution)/shard_map/ppermute | solution.py:39
  54.7 21.2 %collective-permute-start.14 = (bf16[4,2,64,512]{3,2,1,0:T(8,128)(2,1)}, bf16[4,2,64,512]{3,2,1,0:T(8,128)(2,1)S(1)}, u32[]{:S(2)}, u32[]{:S(2)}) collective-permute-start(bf16[4,2,64,512]{3,2,1,0:T(8,128)(2,1)} %get-tuple-element.99.refs_0_), channel_id=1, source_target_pairs={{0,4},{2,6},{4,0},{6,2},{8,12},{10,14},{12,8},{14,10},{16,20},{18,... | collective-permute-start | bytes 1572872 | tf_op jit(solution)/shard_map/ppermute | solution.py:34
  58.0 19.2 %collective-permute-start.15 = (bf16[4,2,64,512]{3,2,1,0:T(8,128)(2,1)}, bf16[4,2,64,512]{3,2,1,0:T(8,128)(2,1)S(1)}, u32[]{:S(2)}, u32[]{:S(2)}) collective-permute-start(bf16[4,2,64,512]{3,2,1,0:T(8,128)(2,1)} %get-tuple-element.100.refs_2_), channel_id=1, source_target_pairs={{0,2},{2,0},{4,6},{6,4},{8,10},{10,8},{12,14},{14,12},{16,18},{18,... | collective-permute-start | bytes 1572872 | tf_op jit(solution)/shard_map/ppermute | solution.py:34
  66.8 15.9 %collective-permute-start.19 = (bf16[4,64,512]{2,1,0:T(8,128)(2,1)}, bf16[4,64,512]{2,1,0:T(8,128)(2,1)}, u32[]{:S(2)}, u32[]{:S(2)}) collective-permute-start(bf16[4,64,512]{2,1,0:T(8,128)(2,1)} %get-tuple-element.113.refs_0_), channel_id=1, source_target_pairs={{0,2},{2,0},{4,6},{6,4},{8,10},{10,8},{12,14},{14,12},{16,18},{18,... | collective-permute-start | bytes 786440 | tf_op jit(solution)/shard_map/ppermute | solution.py:34
  67.3 15.4 %collective-permute-start.20 = (bf16[4,64,512]{2,1,0:T(8,128)(2,1)}, bf16[4,64,512]{2,1,0:T(8,128)(2,1)}, u32[]{:S(2)}, u32[]{:S(2)}) collective-permute-start(bf16[4,64,512]{2,1,0:T(8,128)(2,1)} %get-tuple-element.114.refs_2_), channel_id=1, source_target_pairs={{0,4},{2,6},{4,0},{6,2},{8,12},{10,14},{12,8},{14,10},{16,20},{18,... | collective-permute-start | bytes 786440 | tf_op jit(solution)/shard_map/ppermute | solution.py:34
  75.9 20.7 %collective-permute-start.13 = (bf16[4,2,64,768]{3,2,1,0:T(8,128)(2,1)}, bf16[4,2,64,768]{3,2,1,0:T(8,128)(2,1)}, u32[]{:S(2)}, u32[]{:S(2)}) collective-permute-start(bf16[4,2,64,768]{3,2,1,0:T(8,128)(2,1)} %get-tuple-element.95.refs_2_), channel_id=1, source_target_pairs={{0,2},{2,0},{4,6},{6,4},{8,10},{10,8},{12,14},{14,12},{16,18},{18,... | collective-permute-start | bytes 2359304 | tf_op jit(solution)/shard_map/ppermute | solution.py:34
  77.3 19.1 %collective-permute-start.12 = (bf16[4,2,64,640]{3,2,1,0:T(8,128)(2,1)}, bf16[4,2,64,640]{3,2,1,0:T(8,128)(2,1)}, u32[]{:S(2)}, u32[]{:S(2)}) collective-permute-start(bf16[4,2,64,640]{3,2,1,0:T(8,128)(2,1)} %get-tuple-element.94.refs_0_), channel_id=1, source_target_pairs={{0,4},{2,6},{4,0},{6,2},{8,12},{10,14},{12,8},{14,10},{16,20},{18,... | collective-permute-start | bytes 1966088 | tf_op jit(solution)/shard_map/ppermute | solution.py:34
  86.2 29.8 %collective-permute-start.21 = (bf16[4,2,64,512]{3,2,1,0:T(8,128)(2,1)}, bf16[4,2,64,512]{3,2,1,0:T(8,128)(2,1)}, u32[]{:S(2)}, u32[]{:S(2)}) collective-permute-start(bf16[4,2,64,512]{3,2,1,0:T(8,128)(2,1)} %get-tuple-element.115.refs_0_), channel_id=1, source_target_pairs={{0,4},{2,6},{4,0},{6,2},{8,12},{10,14},{12,8},{14,10},{16,20},{18,... | collective-permute-start | bytes 1572872 | tf_op jit(solution)/shard_map/ppermute | solution.py:34
  86.9 29.0 %collective-permute-start.22 = (bf16[4,2,64,512]{3,2,1,0:T(8,128)(2,1)}, bf16[4,2,64,512]{3,2,1,0:T(8,128)(2,1)}, u32[]{:S(2)}, u32[]{:S(2)}) collective-permute-start(bf16[4,2,64,512]{3,2,1,0:T(8,128)(2,1)} %get-tuple-element.116.refs_2_), channel_id=1, source_target_pairs={{0,2},{2,0},{4,6},{6,4},{8,10},{10,8},{12,14},{14,12},{16,18},{18,... | collective-permute-start | bytes 1572872 | tf_op jit(solution)/shard_map/ppermute | solution.py:34
  194.4 17.8 %collective-permute-start.26 = (bf16[512,640]{1,0:T(8,128)(2,1)}, bf16[512,640]{1,0:T(8,128)(2,1)S(1)}, u32[]{:S(2)}, u32[]{:S(2)}) collective-permute-start(bf16[512,640]{1,0:T(8,128)(2,1)} %get-tuple-element.138), channel_id=1, source_target_pairs={{0,4},{2,6},{4,0},{6,2},{8,12},{10,14},{12,8},{14,10},{16,20},{18,... | collective-permute-start | bytes 1966088 | tf_op jit(solution)/shard_map/ppermute | solution.py:34
  195.9 20.6 %collective-permute-start.28 = (bf16[512,768]{1,0:T(8,128)(2,1)}, bf16[512,768]{1,0:T(8,128)(2,1)S(1)}, u32[]{:S(2)}, u32[]{:S(2)}) collective-permute-start(bf16[512,768]{1,0:T(8,128)(2,1)} %get-tuple-element.140), channel_id=1, source_target_pairs={{0,2},{2,0},{4,6},{6,4},{8,10},{10,8},{12,14},{14,12},{16,18},{18,... | collective-permute-start | bytes 2359304 | tf_op jit(solution)/shard_map/ppermute | solution.py:34
  196.4 49.1 %collective-permute-start.38 = (bf16[512,1024]{1,0:T(8,128)(2,1)}, bf16[512,1024]{1,0:T(8,128)(2,1)S(1)}, u32[]{:S(2)}, u32[]{:S(2)}) collective-permute-start(bf16[512,1024]{1,0:T(8,128)(2,1)} %get-tuple-element.151), channel_id=1, source_target_pairs={{0,2},{2,0},{4,6},{6,4},{8,10},{10,8},{12,14},{14,12},{16,18},{18,... | collective-permute-start | bytes 3145736 | tf_op jit(solution)/shard_map/ppermute | solution.py:34
  197.9 50.4 %collective-permute-start.36 = (bf16[512,1024]{1,0:T(8,128)(2,1)}, bf16[512,1024]{1,0:T(8,128)(2,1)S(1)}, u32[]{:S(2)}, u32[]{:S(2)}) collective-permute-start(bf16[512,1024]{1,0:T(8,128)(2,1)} %get-tuple-element.149), channel_id=1, source_target_pairs={{0,4},{2,6},{4,0},{6,2},{8,12},{10,14},{12,8},{14,10},{16,20},{18,... | collective-permute-start | bytes 3145736 | tf_op jit(solution)/shard_map/ppermute | solution.py:34
  199.7 64.1 %collective-permute-start.24 = (f32[256,1024]{1,0:T(8,128)S(1)}, f32[256,1024]{1,0:T(8,128)S(1)}, u32[]{:S(2)}, u32[]{:S(2)}) collective-permute-start(f32[256,1024]{1,0:T(8,128)S(1)} %pad_maximum_fusion.4), channel_id=1, source_target_pairs={{0,1},{1,0},{2,3},{3,2},{4,5},{5,4},{6,7},{7,6},{8,9},{9,8},{10,11... | collective-permute-start | bytes 3145736 | tf_op jit(solution)/shard_map/ppermute | solution.py:44
  212.2 38.0 %collective-permute-start.25 = (f32[256,1024]{1,0:T(8,128)S(1)}, f32[256,1024]{1,0:T(8,128)S(1)}, u32[]{:S(2)}, u32[]{:S(2)}) collective-permute-start(f32[256,1024]{1,0:T(8,128)S(1)} %copy-done.55), channel_id=1, source_target_pairs={{0,1},{1,0},{2,3},{3,2},{4,5},{5,4},{6,7},{7,6},{8,9},{9,8},{10,11... | collective-permute-start | bytes 3145736 | tf_op jit(solution)/shard_map/ppermute | solution.py:44
  216.5 28.4 %collective-permute-start.27 = (bf16[4,64,640]{2,1,0:T(8,128)(2,1)S(1)}, bf16[4,64,640]{2,1,0:T(8,128)(2,1)S(1)}, u32[]{:S(2)}, u32[]{:S(2)}) collective-permute-start(bf16[4,64,640]{2,1,0:T(8,128)(2,1)S(1)} %fusion.26), channel_id=1, source_target_pairs={{0,2},{2,0},{4,6},{6,4},{8,10},{10,8},{12,14},{14,12},{16,18},{18,... | collective-permute-start | bytes 983048 | tf_op jit(solution)/shard_map/ppermute | solution.py:34
  244.9 23.1 %collective-permute-start.29 = (bf16[4,64,768]{2,1,0:T(8,128)(2,1)S(1)}, bf16[4,64,768]{2,1,0:T(8,128)(2,1)S(1)}, u32[]{:S(2)}, u32[]{:S(2)}) collective-permute-start(bf16[4,64,768]{2,1,0:T(8,128)(2,1)S(1)} %fusion.20), channel_id=1, source_target_pairs={{0,4},{2,6},{4,0},{6,2},{8,12},{10,14},{12,8},{14,10},{16,20},{18,... | collective-permute-start | bytes 1179656 | tf_op jit(solution)/shard_map/ppermute | solution.py:34
  246.9 56.7 %collective-permute-start.39 = (bf16[4,64,1024]{2,1,0:T(8,128)(2,1)}, bf16[4,64,1024]{2,1,0:T(8,128)(2,1)}, u32[]{:S(2)}, u32[]{:S(2)}) collective-permute-start(bf16[4,64,1024]{2,1,0:T(8,128)(2,1)} %fusion.8), channel_id=1, source_target_pairs={{0,4},{2,6},{4,0},{6,2},{8,12},{10,14},{12,8},{14,10},{16,20},{18,... | collective-permute-start | bytes 1572872 | tf_op jit(solution)/shard_map/ppermute | solution.py:34
  249.7 55.0 %collective-permute-start.37 = (bf16[4,64,1024]{2,1,0:T(8,128)(2,1)}, bf16[4,64,1024]{2,1,0:T(8,128)(2,1)}, u32[]{:S(2)}, u32[]{:S(2)}) collective-permute-start(bf16[4,64,1024]{2,1,0:T(8,128)(2,1)} %fusion.9), channel_id=1, source_target_pairs={{0,2},{2,0},{4,6},{6,4},{8,10},{10,8},{12,14},{14,12},{16,18},{18,... | collective-permute-start | bytes 1572872 | tf_op jit(solution)/shard_map/ppermute | solution.py:34
  250.7 12.5 %collective-permute-start.33 = (f32[96,128]{1,0:T(8,128)S(1)}, f32[96,128]{1,0:T(8,128)S(1)}, u32[]{:S(2)}, u32[]{:S(2)}) collective-permute-start(f32[96,128]{1,0:T(8,128)S(1)} %constant_dynamic-update-slice_fusion), channel_id=1, source_target_pairs={{0,2},{2,0},{4,6},{6,4},{8,10},{10,8},{12,14},{14,12},{16,18},{18,... | collective-permute-start | bytes 147464 | tf_op jit(solution)/shard_map/ppermute | solution.py:34
  274.0 29.6 %collective-permute-start.32 = (bf16[64,1408]{1,0:T(8,128)(2,1)}, bf16[64,1408]{1,0:T(8,128)(2,1)}, u32[]{:S(2)}, u32[]{:S(2)}) collective-permute-start(bf16[64,1408]{1,0:T(8,128)(2,1)} %get-tuple-element.166), channel_id=1, source_target_pairs={{0,24},{2,26},{4,28},{6,30},{8,0},{10,2},{12,4},{14,6},{16,8},{18,... | collective-permute-start | bytes 540680 | tf_op jit(solution)/shard_map/ppermute | solution.py:39
  276.1 27.4 %collective-permute-start.31 = (bf16[64,1408]{1,0:T(8,128)(2,1)}, bf16[64,1408]{1,0:T(8,128)(2,1)}, u32[]{:S(2)}, u32[]{:S(2)}) collective-permute-start(bf16[64,1408]{1,0:T(8,128)(2,1)} %get-tuple-element.167), channel_id=1, source_target_pairs={{0,16},{2,18},{4,20},{6,22},{8,24},{10,26},{12,28},{14,30},{16,0},... | collective-permute-start | bytes 540680 | tf_op jit(solution)/shard_map/ppermute | solution.py:39
  286.8 16.8 %collective-permute-start.30 = (bf16[64,1408]{1,0:T(8,128)(2,1)}, bf16[64,1408]{1,0:T(8,128)(2,1)}, u32[]{:S(2)}, u32[]{:S(2)}) collective-permute-start(bf16[64,1408]{1,0:T(8,128)(2,1)} %get-tuple-element.168), channel_id=1, source_target_pairs={{0,8},{2,10},{4,12},{6,14},{8,16},{10,18},{12,20},{14,22},{16,24},... | collective-permute-start | bytes 540680 | tf_op jit(solution)/shard_map/ppermute | solution.py:39
  308.2 19.9 %collective-permute-start.41 = (bf16[64,2048]{1,0:T(8,128)(2,1)S(1)}, bf16[64,2048]{1,0:T(8,128)(2,1)S(1)}, u32[]{:S(2)}, u32[]{:S(2)}) collective-permute-start(bf16[64,2048]{1,0:T(8,128)(2,1)S(1)} %get-tuple-element.162), channel_id=1, source_target_pairs={{0,16},{2,18},{4,20},{6,22},{8,24},{10,26},{12,28},{14,30},{16,0},... | collective-permute-start | bytes 786440 | tf_op jit(solution)/shard_map/ppermute | solution.py:39
  311.6 22.0 %collective-permute-start.40 = (bf16[64,2048]{1,0:T(8,128)(2,1)S(1)}, bf16[64,2048]{1,0:T(8,128)(2,1)S(1)}, u32[]{:S(2)}, u32[]{:S(2)}) collective-permute-start(bf16[64,2048]{1,0:T(8,128)(2,1)S(1)} %get-tuple-element.163), channel_id=1, source_target_pairs={{0,8},{2,10},{4,12},{6,14},{8,16},{10,18},{12,20},{14,22},{16,24},... | collective-permute-start | bytes 786440 | tf_op jit(solution)/shard_map/ppermute | solution.py:39
  314.4 24.1 %collective-permute-start.35 = (f32[32,1408]{1,0:T(8,128)S(1)}, f32[32,1408]{1,0:T(8,128)S(1)}, u32[]{:S(2)}, u32[]{:S(2)}) collective-permute-start(f32[32,1408]{1,0:T(8,128)S(1)} %get-tuple-element.171), channel_id=1, source_target_pairs={{0,1},{1,0},{2,3},{3,2},{4,5},{5,4},{6,7},{7,6},{8,9},{9,8},{10,11... | collective-permute-start | bytes 540680 | tf_op jit(solution)/shard_map/ppermute | solution.py:44
  (74 other events, 650.1 us)
